TPU v7x, 32 devices: a whole 2x2x4 slice. The times are simulated.
32 devices in a mesh: groups: 2 (over y), seq: 4 (over z), head: 4 (over x, core).
Axes of the slice: x: 2, y: 2, z: 4, core: 2. Of those that a mesh axis runs over, the one named last changes fastest.
Arguments:
- tokens: bfloat16 [8192, 2048], P(('groups', 'seq'), 'head'), parts along dimension 0, may hold values from -6 to 6
- q_weight: bfloat16 [2048, 2048], P(None, 'head'), may hold values from -0.125 to 0.125
- k_weight: bfloat16 [2048, 2048], P(None, 'head'), may hold values from -0.125 to 0.125
- v_weight: bfloat16 [2048, 2048], P(None, 'head'), may hold values from -0.125 to 0.125
- level_table: float32 [16, 16], P('head'), may hold values from 0.1 to 1
- level_index: int32 [6, 8192], P(None, ('groups', 'seq')), parts along dimension 1, may hold values from 0 to 15
- out_gain: float32 [2048], P('head'), may hold values from 0.5 to 1.5
Outputs:
- attended: bfloat16 [8192, 2048], P(('groups', 'seq'), 'head'), parts along dimension 0
There are 2 independent parts, one for each index of `groups`. A program takes and returns all parts, laid end to end along the dimension named above; an argument that names none is the same for every part. Nothing has to cross between parts.
Inputs may be any that keep to these rules, and one draw needn't show every extreme that they name: `level_index`: row 0 weights a token's own block, row l + 1 its level-l merged state.
All inputs are finite; a program needn't handle non-finite values.
Results may differ from a plain program's by a relative error of at most 0.012.
Values may be sent and summed in bfloat16 or wider, within the bound.
No kernel may reach another device: no remote copies, remote signals or barrier semaphores. Data moves between devices by JAX's collectives and lax.ppermute only.
A program may use at most 64 MiB of HBM per device.

v0:
```python
import functools

import jax
import jax.numpy as jnp
from jax import lax
from jax.experimental import pallas as pl
from jax.experimental.pallas import tpu as pltpu
from jax.sharding import PartitionSpec as P


CHUNKS = (2, 2, 2, 1, 1)
EPS = 1e-06
F32 = jnp.float32
BF16 = jnp.bfloat16
VMEM = pl.BlockSpec(memory_space=pltpu.VMEM)
SMEM = pl.BlockSpec(memory_space=pltpu.SMEM)
ANY = pl.BlockSpec(memory_space=pl.ANY)


def swap(block, axis, apart):
    route = [(i, i ^ apart) for i in range(lax.axis_size(axis))]
    return lax.ppermute(block, axis, route)


def dot(a, b, dims=((1,), (0,))):
    return lax.dot_general(a, b, (dims, ((), ())), preferred_element_type=F32)


def call(kernel, outs, in_specs, args, out_specs=None, scratch=(), limit=8):
    return pl.pallas_call(
        kernel,
        out_shape=[jax.ShapeDtypeStruct(*out) for out in outs],
        in_specs=in_specs,
        out_specs=out_specs or [VMEM] * len(outs),
        scratch_shapes=scratch,
        compiler_params=pltpu.CompilerParams(vmem_limit_bytes=limit << 20),
    )(*args)


def weight_rows(me, weight, offset, depth):
    start = pl.multiple_of((me ^ offset) * depth, depth)
    return weight[pl.ds(start, depth), :]


def unit_rows(raw):
    return (raw * lax.rsqrt(jnp.sum(raw * raw, -1, keepdims=True) + EPS)).astype(BF16)


def cut_kernel(spans, tokens, *refs):
    count = len(spans)
    outs, sems = refs[:count], refs[count]
    copies = []
    for i, (lo, hi) in enumerate(spans):
        copy = pltpu.make_async_copy(tokens.at[lo:hi], outs[i], sems.at[i])
        copy.start()
        copies.append(copy)
    for copy in copies:
        copy.wait()


def early_kernel(n_near, tile, me, *refs):
    pieces = refs[:n_near]
    weights = refs[n_near : n_near + 3]
    sums = refs[n_near + 3 :]
    rows, depth = pieces[0].shape

    def step(i, carry):
        at = pl.ds(pl.multiple_of(i * tile, tile), tile)
        for weight, total in zip(weights, sums):
            acc = None
            for offset, piece in enumerate(pieces):
                part = dot(piece[at, :], weight_rows(me[0], weight, offset, depth))
                acc = part if acc is None else acc + part
            total[at, :] = acc
        return carry

    lax.fori_loop(0, rows // tile, step, 0)


def late_sum(me, base, pieces, weight, early, lo, rows):
    depth = pieces[0].shape[1]
    acc = early[lo : lo + rows, :]
    for offset, piece in enumerate(pieces):
        acc = acc + dot(piece[...], weight_rows(me, weight, base + offset, depth))
    return acc


def kv_kernel(base, lo, heads, me, *refs):
    pieces = refs[:base]
    k_weight, v_weight, k_early, v_early = refs[base : base + 4]
    state_in = refs[base + 4] if lo else None
    keys, values, state, state_low = refs[-4:]
    rows, width = keys.shape
    size = width // heads
    raw_v = late_sum(me[0], base, pieces, v_weight, v_early, lo, rows).astype(BF16)
    values[...] = raw_v
    raw_k = late_sum(me[0], base, pieces, k_weight, k_early, lo, rows)
    for head in range(heads):
        cols = slice(head * size, (head + 1) * size)
        key = unit_rows(raw_k[:, cols])
        keys[:, cols] = key
        total = dot(key, raw_v[:, cols], ((0,), (0,)))
        if lo:
            total = state_in[head] + total
        state[head] = total
        state_low[head] = total.astype(BF16)


def table_kernel(table, wide):
    heads, _ = table.shape
    width = wide.shape[1]
    size = width // heads
    row = lax.broadcasted_iota(jnp.int32, (heads, width), 0)
    col = lax.broadcasted_iota(jnp.int32, (heads, width), 1)
    mine = ((col >= row * size) & (col < (row + 1) * size)).astype(BF16)
    exact = table[...]
    high = exact.astype(BF16)
    low = (exact - high.astype(F32)).astype(BF16)
    both = [dot(part, mine, ((0,), (0,))).astype(BF16) for part in (high, low)]
    wide[...] = jnp.concatenate(both, 0)


def level_weights(depth, block, index, table):
    quant = table.shape[0] // 2
    levels, rows = index.shape
    spot = lax.broadcasted_iota(jnp.int32, (quant, rows), 0)

    def picked(level):
        return (index[level : level + 1, :] == spot).astype(F32)

    def weigh(hot):
        hot = hot.astype(BF16)
        return dot(jnp.concatenate([hot, hot], 0), table[...], ((0,), (0,)))

    rest = jnp.zeros((quant, rows), F32)
    for level in range(depth + 1, levels):
        rest = rest + picked(level)
    far = [weigh(picked(level + 1)) * (block >> level & 1).astype(F32) for level in range(depth)]
    return weigh(picked(0)), weigh(rest), far


def query_kernel(base, lo, heads, depth, me, block, *refs):
    pieces = refs[:base]
    q_weight, q_early, keys, values, index, table = refs[base : base + 6]
    state_in = refs[base + 6] if lo else None
    part = refs[-1 - depth]
    scaled = refs[-depth:]
    rows, width = keys.shape
    size = width // heads
    own, rest, far = level_weights(depth, block[0], index[:, lo : lo + rows], table)
    raw_q = late_sum(me[0], base, pieces, q_weight, q_early, lo, rows)
    causal = lax.broadcasted_iota(jnp.int32, (rows, rows), 0) >= lax.broadcasted_iota(jnp.int32, (rows, rows), 1)
    for head in range(heads):
        cols = slice(head * size, (head + 1) * size)
        query = unit_rows(raw_q[:, cols])
        scores = dot(query, keys[:, cols], ((1,), (1,)))
        scores = jnp.where(causal, scores, 0.0).astype(BF16)
        local = dot(scores, values[:, cols])
        if lo:
            local = local + dot(query, state_in[head].astype(BF16))
        wide = query.astype(F32)
        empty = (wide * rest[:, cols]).astype(BF16)
        part[:, cols] = own[:, cols] * local + dot(empty, jnp.zeros((size, size), BF16))
        for level in range(depth):
            scaled[level][:, cols] = (wide * far[level][:, cols]).astype(BF16)


def add_kernel(total, partner, grown, low):
    summed = total[...] + partner[...].astype(F32)
    grown[...] = summed
    low[...] = summed.astype(BF16)


def final_kernel(heads, depth, edges, *refs):
    count = len(edges) - 1
    parts = refs[:count]
    scaled = [refs[count * (1 + level) : count * (2 + level)] for level in range(depth)]
    refs = refs[count * (1 + depth) :]
    merged = refs[:depth]
    gain, out, done, sems = refs[depth:]
    size = done.shape[1] // heads
    copies = []
    for i in range(count):
        rows = slice(edges[i], edges[i + 1])
        for head in range(heads):
            cols = slice(head * size, (head + 1) * size)
            total = parts[i][:, cols]
            for level in range(depth):
                total = total + dot(scaled[level][i][:, cols], merged[level][head])
            total = total * lax.rsqrt(jnp.mean(total * total, -1, keepdims=True) + EPS)
            done[rows, cols] = (total * gain[0:1, cols]).astype(BF16)
        copy = pltpu.make_async_copy(done.at[rows], out.at[rows], sems.at[i])
        copy.start()
        copies.append(copy)
    for copy in copies:
        copy.wait()


def hop(piece, base):
    pieces = [piece]
    apart = 1
    while apart < base:
        pieces += [swap(piece, "head", apart) for piece in pieces]
        apart *= 2
    return pieces


def on_device(tokens, q_weight, k_weight, v_weight, level_table, level_index, out_gain):
    row_count, feat_here = tokens.shape
    width = q_weight.shape[1]
    heads, quant = level_table.shape
    size = width // heads
    base = lax.axis_size("head") // 2
    depth = lax.axis_size("seq").bit_length() - 1
    me = lax.axis_index("head").astype(jnp.int32).reshape(1)
    block = lax.axis_index("seq").astype(jnp.int32).reshape(1)

    unit = row_count // sum(CHUNKS)
    edges = [0]
    for share in CHUNKS:
        edges.append(edges[-1] + share * unit)
    spans = list(zip(edges[:-1], edges[1:]))

    cuts = []
    for group in (spans[:1], spans[1:]):
        cuts += call(
            functools.partial(cut_kernel, group),
            [((hi - lo, feat_here), BF16) for lo, hi in group],
            [ANY],
            (tokens,),
            scratch=[pltpu.SemaphoreType.DMA((len(group),))],
        )
    far = [swap(piece, "head", base) for piece in cuts]
    near = hop(tokens, base)

    big = (row_count, width)
    early = call(
        functools.partial(early_kernel, base, row_count // 4),
        [(big, F32)] * 3,
        [SMEM] + [VMEM] * (base + 3),
        (me, *near, q_weight, k_weight, v_weight),
    )
    table = call(table_kernel, [((2 * quant, width), BF16)], [VMEM], (level_table,))[0]

    state = []
    parts = []
    scaled = []
    for i, (lo, hi) in enumerate(spans):
        rows = hi - lo
        pieces = hop(far[i], base)
        before = state
        args = (me, *pieces, k_weight, v_weight, early[1], early[2], *before)
        keys, values, total, low = call(
            functools.partial(kv_kernel, base, lo, heads),
            [((rows, width), BF16)] * 2 + [((heads, size, size), F32), ((heads, size, size), BF16)],
            [SMEM] + [VMEM] * (len(args) - 1),
            args,
        )
        state = [total]
        args = (me, block, *pieces, q_weight, early[0], keys, values, level_index, table, *before)
        outs = call(
            functools.partial(query_kernel, base, lo, heads, depth),
            [((rows, width), F32)] + [((rows, width), BF16)] * depth,
            [SMEM, SMEM] + [VMEM] * (len(args) - 2),
            args,
        )
        parts.append(outs[0])
        scaled.append(outs[1:])

    merged = []
    for level in range(depth):
        partner = swap(low, "seq", 1 << level)
        merged.append(partner)
        if level + 1 < depth:
            shape = (heads, size, size)
            total, low = call(add_kernel, [(shape, F32), (shape, BF16)], [VMEM, VMEM], (total, partner))

    inputs = parts + [chunk[level] for level in range(depth) for chunk in scaled] + merged
    return call(
        functools.partial(final_kernel, heads, depth, edges),
        [(big, BF16)],
        [VMEM] * (len(inputs) + 1),
        (*inputs, out_gain.reshape(1, width)),
        out_specs=[ANY],
        scratch=[pltpu.VMEM(big, BF16), pltpu.SemaphoreType.DMA((len(spans),))],
    )[0]


def solution(mesh):
    return jax.shard_map(
        on_device,
        mesh=mesh,
        in_specs=(
            P(("groups", "seq"), "head"),
            P(None, "head"),
            P(None, "head"),
            P(None, "head"),
            P("head", None),
            P(None, ("groups", "seq")),
            P("head"),
        ),
        out_specs=P(("groups", "seq"), "head"),
        check_vma=False,
    )
```

profile of v0, /device:TPU:0, one launch (start us, length us, event | category | flops | bytes accessed | tf_op | source)
XLA Modules:
  0.0 85.6 jit_solution(7071226574009218742)
XLA Ops:
  0.0 0.5 collective-permute-start.2
  0.5 1.4 %copy-done.7 = bf16[1024,512]{1,0:T(8,128)(2,1)S(1)} copy-done((bf16[1024,512]{1,0:T(8,128)(2,1)S(1)}, bf16[1024,512]{1,0:T(8,128)(2,1)}, u32[]{:S(2)}) %copy-start.7) | copy-done | bytes 1048600
  1.9 2.6 %collective-permute-start = (bf16[256,512]{1,0:T(8,128)(2,1)S(1)}, bf16[256,512]{1,0:T(8,128)(2,1)}, u32[]{:S(2)}, u32[]{:S(2)}) collective-permute-start(bf16[256,512]{1,0:T(8,128)(2,1)S(1)} %shard_map.73), channel_id=1, source_target_pairs={{0,2},{1,3},{2,0},{3,1},{4,6},{5,7},{6,4},{7,5},{8,10},{9,11},{10,... | collective-permute-start | bytes 786440 | tf_op jit(solution)/shard_map/ppermute | solution.py:22
  4.4 0.4 shard_map.78
  4.9 0.1 collective-permute-start.3
  5.0 2.0 %collective-permute-start.5 = (bf16[256,512]{1,0:T(8,128)(2,1)S(1)}, bf16[256,512]{1,0:T(8,128)(2,1)S(1)}, u32[]{:S(2)}, u32[]{:S(2)}) collective-permute-start(bf16[256,512]{1,0:T(8,128)(2,1)S(1)} %get-tuple-element.55), channel_id=1, source_target_pairs={{0,2},{1,3},{2,0},{3,1},{4,6},{5,7},{6,4},{7,5},{8,10},{9,11},{10,... | collective-permute-start | bytes 786440 | tf_op jit(solution)/shard_map/ppermute | solution.py:22
  7.0 0.1 collective-permute-start.7
  7.0 4.7 %collective-permute-done.refs_0_ = bf16[256,512]{1,0:T(8,128)(2,1)} collective-permute-done((bf16[256,512]{1,0:T(8,128)(2,1)S(1)}, bf16[256,512]{1,0:T(8,128)(2,1)}, u32[]{:S(2)}, u32[]{:S(2)}) %collective-permute-start) | collective-permute-done | bytes 262176 | tf_op jit(solution)/shard_map/ppermute | solution.py:22
  11.7 5.6 %collective-permute-done.3.refs_0_ = bf16[256,512]{1,0:T(8,128)(2,1)} collective-permute-done((bf16[256,512]{1,0:T(8,128)(2,1)S(1)}, bf16[256,512]{1,0:T(8,128)(2,1)}, u32[]{:S(2)}, u32[]{:S(2)}) %collective-permute-start.3) | collective-permute-done | bytes 262176 | tf_op jit(solution)/shard_map/ppermute | solution.py:22
  17.3 0.0 collective-permute-start.4
  17.3 5.5 %collective-permute-done.5.refs_0_ = bf16[256,512]{1,0:T(8,128)(2,1)S(1)} collective-permute-done((bf16[256,512]{1,0:T(8,128)(2,1)S(1)}, bf16[256,512]{1,0:T(8,128)(2,1)S(1)}, u32[]{:S(2)}, u32[]{:S(2)}) %collective-permute-start.5) | collective-permute-done | bytes 262176 | tf_op jit(solution)/shard_map/ppermute | solution.py:22
  22.8 2.5 %collective-permute-done.7.refs_0_ = bf16[128,512]{1,0:T(8,128)(2,1)S(1)} collective-permute-done((bf16[128,512]{1,0:T(8,128)(2,1)S(1)}, bf16[128,512]{1,0:T(8,128)(2,1)S(1)}, u32[]{:S(2)}, u32[]{:S(2)}) %collective-permute-start.7) | collective-permute-done | bytes 131104 | tf_op jit(solution)/shard_map/ppermute | solution.py:22
  25.3 1.7 %collective-permute-start.9 = (bf16[128,512]{1,0:T(8,128)(2,1)S(1)}, bf16[128,512]{1,0:T(8,128)(2,1)}, u32[]{:S(2)}, u32[]{:S(2)}) collective-permute-start(bf16[128,512]{1,0:T(8,128)(2,1)S(1)} %get-tuple-element.65), channel_id=1, source_target_pairs={{0,2},{1,3},{2,0},{3,1},{4,6},{5,7},{6,4},{7,5},{8,10},{9,11},{10,... | collective-permute-start | bytes 393224 | tf_op jit(solution)/shard_map/ppermute | solution.py:22
  27.1 3.5 %collective-permute-done.9.refs_0_ = bf16[128,512]{1,0:T(8,128)(2,1)} collective-permute-done((bf16[128,512]{1,0:T(8,128)(2,1)S(1)}, bf16[128,512]{1,0:T(8,128)(2,1)}, u32[]{:S(2)}, u32[]{:S(2)}) %collective-permute-start.9) | collective-permute-done | bytes 131104 | tf_op jit(solution)/shard_map/ppermute | solution.py:22
  30.6 0.5 collective-permute-start.10
  31.1 1.6 %copy-done.1 = bf16[2048,512]{1,0:T(8,128)(2,1)S(1)} copy-done((bf16[2048,512]{1,0:T(8,128)(2,1)S(1)}, bf16[2048,512]{1,0:T(8,128)(2,1)}, u32[]{:S(2)}) %copy-start.1) | copy-done | bytes 2097176
  32.7 1.6 %copy-done.3 = bf16[2048,512]{1,0:T(8,128)(2,1)S(1)} copy-done((bf16[2048,512]{1,0:T(8,128)(2,1)S(1)}, bf16[2048,512]{1,0:T(8,128)(2,1)}, u32[]{:S(2)}) %copy-start.3) | copy-done | bytes 2097176
  34.3 1.2 %copy-done.8 = bf16[1024,512]{1,0:T(8,128)(2,1)S(1)} copy-done((bf16[1024,512]{1,0:T(8,128)(2,1)S(1)}, bf16[1024,512]{1,0:T(8,128)(2,1)}, u32[]{:S(2)}) %copy-start.8) | copy-done | bytes 1048600
  35.5 3.9 %shard_map.74 = (f32[1024,512]{1,0:T(8,128)S(1)}, f32[1024,512]{1,0:T(8,128)S(1)}, f32[1024,512]{1,0:T(8,128)S(1)}) custom-call(s32[1]{0:T(128)} %bitcast.me, bf16[1024,512]{1,0:T(8,128)(2,1)S(1)} %copy-done.8, bf16[1024,512]{1,0:T(8,128)(2,1)S(1)} %collective-permute-done.2.refs_1_, bf16[2048,512]{1,0:T(8,128)(2,1)S(1)} %copy-done.3, ...), custom_call_target="tpu_custom_call" | custom-call | tf_op jit(solution)/shard_map/pallas_call | solution.py:30
  39.5 1.3 %copy-done.5 = f32[1024,512]{1,0:T(8,128)} copy-done((f32[1024,512]{1,0:T(8,128)}, f32[1024,512]{1,0:T(8,128)S(1)}, u32[]{:S(2)}) %copy-start.5) | copy-done | bytes 2097176
  40.8 0.0 collective-permute-done.1.refs_1_
  40.8 2.8 %shard_map.75 = (bf16[256,512]{1,0:T(8,128)(2,1)S(1)}, bf16[256,512]{1,0:T(8,128)(2,1)S(1)}, f32[4,128,128]{2,1,0:T(8,128)S(1)}, bf16[4,128,128]{2,1,0:T(8,128)(2,1)}) custom-call(s32[1]{0:T(128)} %bitcast.me, bf16[256,512]{1,0:T(8,128)(2,1)} %collective-permute-done.refs_0_, bf16[256,512]{1,0:T(8,128)(2,1)} %collective-permute-done.1.refs_1_, ...), custom_call_target="tpu_custom_call" | custom-call | tf_op jit(solution)/shard_map/pallas_call | solution.py:30
  43.7 0.7 copy-done.20
  44.4 0.7 copy-done.22
  45.1 2.8 %shard_map.79 = (bf16[256,512]{1,0:T(8,128)(2,1)S(1)}, bf16[256,512]{1,0:T(8,128)(2,1)S(1)}, f32[4,128,128]{2,1,0:T(8,128)S(1)}, bf16[4,128,128]{2,1,0:T(8,128)(2,1)}) custom-call(s32[1]{0:T(128)} %bitcast.me, bf16[256,512]{1,0:T(8,128)(2,1)} %collective-permute-done.3.refs_0_, bf16[256,512]{1,0:T(8,128)(2,1)} %collective-permute-done.4.refs_1_, ...), custom_call_target="tpu_custom_call" | custom-call | tf_op jit(solution)/shard_map/pallas_call | solution.py:30
  47.9 0.7 copy-done.16
  48.6 2.8 %shard_map.81 = (bf16[256,512]{1,0:T(8,128)(2,1)S(1)}, bf16[256,512]{1,0:T(8,128)(2,1)S(1)}, f32[4,128,128]{2,1,0:T(8,128)S(1)}, bf16[4,128,128]{2,1,0:T(8,128)(2,1)}) custom-call(s32[1]{0:T(128)} %bitcast.me, bf16[256,512]{1,0:T(8,128)(2,1)S(1)} %collective-permute-done.5.refs_0_, bf16[256,512]{1,0:T(8,128)(2,1)} %collective-permute-done.6.refs_1_, ...), custom_call_target="tpu_custom_call" | custom-call | tf_op jit(solution)/shard_map/pallas_call | solution.py:30
  51.4 0.7 copy-done.14
  52.1 2.4 %shard_map.83 = (bf16[128,512]{1,0:T(8,128)(2,1)S(1)}, bf16[128,512]{1,0:T(8,128)(2,1)S(1)}, f32[4,128,128]{2,1,0:T(8,128)S(1)}, bf16[4,128,128]{2,1,0:T(8,128)(2,1)}) custom-call(s32[1]{0:T(128)} %bitcast.me, bf16[128,512]{1,0:T(8,128)(2,1)S(1)} %collective-permute-done.7.refs_0_, bf16[128,512]{1,0:T(8,128)(2,1)} %collective-permute-done.8.refs_1_, ...), custom_call_target="tpu_custom_call" | custom-call | tf_op jit(solution)/shard_map/pallas_call | solution.py:30
  54.6 0.6 copy-done.28
  55.2 0.7 copy-done.30
  55.9 1.7 %shard_map.85 = (bf16[128,512]{1,0:T(8,128)(2,1)S(1)}, bf16[128,512]{1,0:T(8,128)(2,1)S(1)}, f32[4,128,128]{2,1,0:T(8,128)S(1)}, bf16[4,128,128]{2,1,0:T(8,128)(2,1)S(1)}) custom-call(s32[1]{0:T(128)} %bitcast.me, bf16[128,512]{1,0:T(8,128)(2,1)} %collective-permute-done.9.refs_0_, bf16[128,512]{1,0:T(8,128)(2,1)} %collective-permute-done.10.refs_1_, ...), custom_call_target="tpu_custom_call" | custom-call | tf_op jit(solution)/shard_map/pallas_call | solution.py:30
  57.6 1.7 %collective-permute-start.11 = (bf16[4,128,128]{2,1,0:T(8,128)(2,1)S(1)}, bf16[4,128,128]{2,1,0:T(8,128)(2,1)S(1)}, u32[]{:S(2)}, u32[]{:S(2)}) collective-permute-start(bf16[4,128,128]{2,1,0:T(8,128)(2,1)S(1)} %get-tuple-element.80), channel_id=1, source_target_pairs={{0,4},{4,0},{8,12},{12,8},{1,5},{5,1},{9,13},{13,9},{2,6},{6,2},{1... | collective-permute-start | bytes 393224 | tf_op jit(solution)/shard_map/ppermute | solution.py:22
  59.3 3.8 %collective-permute-done.11.partner.refs_15_ = bf16[4,128,128]{2,1,0:T(8,128)(2,1)S(1)} collective-permute-done((bf16[4,128,128]{2,1,0:T(8,128)(2,1)S(1)}, bf16[4,128,128]{2,1,0:T(8,128)(2,1)S(1)}, u32[]{:S(2)}, u32[]{:S(2)}) %collective-permute-start.11) | collective-permute-done | bytes 131104 | tf_op jit(solution)/shard_map/ppermute | solution.py:22
  63.1 0.7 shard_map.87
  63.9 2.6 %collective-permute-start.12 = (bf16[4,128,128]{2,1,0:T(8,128)(2,1)S(1)}, bf16[4,128,128]{2,1,0:T(8,128)(2,1)S(1)}, u32[]{:S(2)}, u32[]{:S(2)}) collective-permute-start(bf16[4,128,128]{2,1,0:T(8,128)(2,1)S(1)} %get-tuple-element.82), channel_id=1, source_target_pairs={{0,8},{4,12},{8,0},{12,4},{1,9},{5,13},{9,1},{13,5},{2,10},{6,14},... | collective-permute-start | bytes 393224 | tf_op jit(solution)/shard_map/ppermute | solution.py:22
  66.5 0.2 shard_map.76.refs_7_
  66.7 1.6 %copy-done.4 = bf16[2048,512]{1,0:T(8,128)(2,1)S(1)} copy-done((bf16[2048,512]{1,0:T(8,128)(2,1)S(1)}, bf16[2048,512]{1,0:T(8,128)(2,1)}, u32[]{:S(2)}) %copy-start.4) | copy-done | bytes 2097176
  68.3 1.6 %copy-done.6 = f32[1024,512]{1,0:T(8,128)S(1)} copy-done((f32[1024,512]{1,0:T(8,128)S(1)}, f32[1024,512]{1,0:T(8,128)}, u32[]{:S(2)}) %copy-start.6) | copy-done | bytes 2097176
  69.9 0.9 %copy-done.21 = bf16[256,512]{1,0:T(8,128)(2,1)S(1)} copy-done((bf16[256,512]{1,0:T(8,128)(2,1)S(1)}, bf16[256,512]{1,0:T(8,128)(2,1)}, u32[]{:S(2)}) %copy-start.21) | copy-done | bytes 262168
  70.8 0.9 %copy-done.23 = bf16[256,512]{1,0:T(8,128)(2,1)S(1)} copy-done((bf16[256,512]{1,0:T(8,128)(2,1)S(1)}, bf16[256,512]{1,0:T(8,128)(2,1)}, u32[]{:S(2)}) %copy-start.23) | copy-done | bytes 262168
  71.8 2.8 %shard_map.77 = (f32[256,512]{1,0:T(8,128)S(1)}, bf16[256,512]{1,0:T(8,128)(2,1)S(1)}, bf16[256,512]{1,0:T(8,128)(2,1)S(1)}) custom-call(s32[1]{0:T(128)} %bitcast.me, s32[1]{0:T(128)} %bitcast.1.block, bf16[256,512]{1,0:T(8,128)(2,1)} %collective-permute-done.refs_0_, bf16[256,512]{1,0:T(8,128)(2,1)} %collective-permute-done.1.refs_1_, ...), custom_call_target="tpu_custom_call" | custom-call | tf_op jit(solution)/shard_map/pallas_call | solution.py:30
  74.6 2.6 %shard_map.80 = (f32[256,512]{1,0:T(8,128)S(1)}, bf16[256,512]{1,0:T(8,128)(2,1)S(1)}, bf16[256,512]{1,0:T(8,128)(2,1)S(1)}) custom-call(s32[1]{0:T(128)} %bitcast.me, s32[1]{0:T(128)} %bitcast.1.block, bf16[256,512]{1,0:T(8,128)(2,1)} %collective-permute-done.3.refs_0_, bf16[256,512]{1,0:T(8,128)(2,1)} %collective-permute-done.4.refs_1_, ...), custom_call_target="tpu_custom_call" | custom-call | tf_op jit(solution)/shard_map/pallas_call | solution.py:30
  77.2 2.5 %shard_map.82 = (f32[256,512]{1,0:T(8,128)S(1)}, bf16[256,512]{1,0:T(8,128)(2,1)S(1)}, bf16[256,512]{1,0:T(8,128)(2,1)S(1)}) custom-call(s32[1]{0:T(128)} %bitcast.me, s32[1]{0:T(128)} %bitcast.1.block, bf16[256,512]{1,0:T(8,128)(2,1)S(1)} %collective-permute-done.5.refs_0_, bf16[256,512]{1,0:T(8,128)(2,1)} %collective-permute-done.6.refs_1_, ...), custom_call_target="tpu_custom_call" | custom-call | tf_op jit(solution)/shard_map/pallas_call | solution.py:30
  79.7 2.1 %shard_map.84 = (f32[128,512]{1,0:T(8,128)S(1)}, bf16[128,512]{1,0:T(8,128)(2,1)S(1)}, bf16[128,512]{1,0:T(8,128)(2,1)S(1)}) custom-call(s32[1]{0:T(128)} %bitcast.me, s32[1]{0:T(128)} %bitcast.1.block, bf16[128,512]{1,0:T(8,128)(2,1)S(1)} %copy-done.11, bf16[128,512]{1,0:T(8,128)(2,1)} %collective-permute-done.8.refs_1_, bf16[2048,512]{1,0:T(8,128)(2,1)S(1)} %copy-done.4, ...), custom_call_target="tpu_custom_call" | custom-call | tf_op jit(solution)/shard_map/pallas_call | solution.py:30
  81.8 0.0 copy-start.32
  81.8 2.1 %shard_map.86 = (f32[128,512]{1,0:T(8,128)S(1)}, bf16[128,512]{1,0:T(8,128)(2,1)S(1)}, bf16[128,512]{1,0:T(8,128)(2,1)S(1)}) custom-call(s32[1]{0:T(128)} %bitcast.me, s32[1]{0:T(128)} %bitcast.1.block, bf16[128,512]{1,0:T(8,128)(2,1)} %collective-permute-done.9.refs_0_, bf16[128,512]{1,0:T(8,128)(2,1)} %collective-permute-done.10.refs_1_, ...), custom_call_target="tpu_custom_call" | custom-call | tf_op jit(solution)/shard_map/pallas_call | solution.py:30
  84.0 1.6 %shard_map.88 = bf16[1024,512]{1,0:T(8,128)(2,1)} custom-call(f32[256,512]{1,0:T(8,128)S(1)} %get-tuple-element.49.refs_0_, f32[256,512]{1,0:T(8,128)S(1)} %get-tuple-element.54.refs_1_, f32[256,512]{1,0:T(8,128)S(1)} %get-tuple-element.59.refs_2_, f32[128,512]{1,0:T(8,128)S(1)} %get-tuple-element.64.refs_3_, f32[128,512]{1,0:T(8,128)S(1)} %get-tuple-element.69.refs_4_, ...), custom_call_target="tpu_custom_call" | custom-call | tf_op jit(solution)/shard_map/pallas_call | solution.py:30
  (62 shorter events, 0.1 us)
Async XLA Ops:
  0.0 31.1 %copy-start = (bf16[2048,512]{1,0:T(8,128)(2,1)S(1)}, bf16[2048,512]{1,0:T(8,128)(2,1)}, u32[]{:S(2)}) copy-start(bf16[2048,512]{1,0:T(8,128)(2,1)} %refs_2_.20) | copy-start | bytes 6291460
  0.0 30.6 %collective-permute-start.2 = (bf16[1024,512]{1,0:T(8,128)(2,1)}, bf16[1024,512]{1,0:T(8,128)(2,1)S(1)}, u32[]{:S(2)}, u32[]{:S(2)}) collective-permute-start(bf16[1024,512]{1,0:T(8,128)(2,1)} %tokens.3), channel_id=1, source_target_pairs={{0,1},{1,0},{2,3},{3,2},{4,5},{5,4},{6,7},{7,6},{8,9},{9,8},{10,11... | collective-permute-start | bytes 3145736 | tf_op jit(solution)/shard_map/ppermute | solution.py:22
  0.5 1.4 %copy-start.7 = (bf16[1024,512]{1,0:T(8,128)(2,1)S(1)}, bf16[1024,512]{1,0:T(8,128)(2,1)}, u32[]{:S(2)}) copy-start(bf16[1024,512]{1,0:T(8,128)(2,1)} %tokens.3) | copy-start | bytes 3145732
  1.9 9.8 %collective-permute-start = (bf16[256,512]{1,0:T(8,128)(2,1)S(1)}, bf16[256,512]{1,0:T(8,128)(2,1)}, u32[]{:S(2)}, u32[]{:S(2)}) collective-permute-start(bf16[256,512]{1,0:T(8,128)(2,1)S(1)} %shard_map.73), channel_id=1, source_target_pairs={{0,2},{1,3},{2,0},{3,1},{4,6},{5,7},{6,4},{7,5},{8,10},{9,11},{10,... | collective-permute-start | bytes 786440 | tf_op jit(solution)/shard_map/ppermute | solution.py:22
  4.9 12.5 %collective-permute-start.3 = (bf16[256,512]{1,0:T(8,128)(2,1)S(1)}, bf16[256,512]{1,0:T(8,128)(2,1)}, u32[]{:S(2)}, u32[]{:S(2)}) collective-permute-start(bf16[256,512]{1,0:T(8,128)(2,1)S(1)} %get-tuple-element.50), channel_id=1, source_target_pairs={{0,2},{1,3},{2,0},{3,1},{4,6},{5,7},{6,4},{7,5},{8,10},{9,11},{10,... | collective-permute-start | bytes 786440 | tf_op jit(solution)/shard_map/ppermute | solution.py:22
  5.0 17.9 %collective-permute-start.5 = (bf16[256,512]{1,0:T(8,128)(2,1)S(1)}, bf16[256,512]{1,0:T(8,128)(2,1)S(1)}, u32[]{:S(2)}, u32[]{:S(2)}) collective-permute-start(bf16[256,512]{1,0:T(8,128)(2,1)S(1)} %get-tuple-element.55), channel_id=1, source_target_pairs={{0,2},{1,3},{2,0},{3,1},{4,6},{5,7},{6,4},{7,5},{8,10},{9,11},{10,... | collective-permute-start | bytes 786440 | tf_op jit(solution)/shard_map/ppermute | solution.py:22
  7.0 18.4 %collective-permute-start.7 = (bf16[128,512]{1,0:T(8,128)(2,1)S(1)}, bf16[128,512]{1,0:T(8,128)(2,1)S(1)}, u32[]{:S(2)}, u32[]{:S(2)}) collective-permute-start(bf16[128,512]{1,0:T(8,128)(2,1)S(1)} %get-tuple-element.60), channel_id=1, source_target_pairs={{0,2},{1,3},{2,0},{3,1},{4,6},{5,7},{6,4},{7,5},{8,10},{9,11},{10,... | collective-permute-start | bytes 393224 | tf_op jit(solution)/shard_map/ppermute | solution.py:22
  11.7 29.1 %collective-permute-start.1 = (bf16[256,512]{1,0:T(8,128)(2,1)}, bf16[256,512]{1,0:T(8,128)(2,1)}, u32[]{:S(2)}, u32[]{:S(2)}) collective-permute-start(bf16[256,512]{1,0:T(8,128)(2,1)} %collective-permute-done.refs_0_), channel_id=1, source_target_pairs={{0,1},{1,0},{2,3},{3,2},{4,5},{5,4},{6,7},{7,6},{8,9},{9,8},{10,11... | collective-permute-start | bytes 786440 | tf_op jit(solution)/shard_map/ppermute | solution.py:22
  17.3 27.7 %collective-permute-start.4 = (bf16[256,512]{1,0:T(8,128)(2,1)}, bf16[256,512]{1,0:T(8,128)(2,1)}, u32[]{:S(2)}, u32[]{:S(2)}) collective-permute-start(bf16[256,512]{1,0:T(8,128)(2,1)} %collective-permute-done.3.refs_0_), channel_id=1, source_target_pairs={{0,1},{1,0},{2,3},{3,2},{4,5},{5,4},{6,7},{7,6},{8,9},{9,8},{10,11... | collective-permute-start | bytes 786440 | tf_op jit(solution)/shard_map/ppermute | solution.py:22
  22.8 25.8 %collective-permute-start.6 = (bf16[256,512]{1,0:T(8,128)(2,1)S(1)}, bf16[256,512]{1,0:T(8,128)(2,1)}, u32[]{:S(2)}, u32[]{:S(2)}) collective-permute-start(bf16[256,512]{1,0:T(8,128)(2,1)S(1)} %collective-permute-done.5.refs_0_), channel_id=1, source_target_pairs={{0,1},{1,0},{2,3},{3,2},{4,5},{5,4},{6,7},{7,6},{8,9},{9,8},{10,11... | collective-permute-start | bytes 786440 | tf_op jit(solution)/shard_map/ppermute | solution.py:22
  25.3 26.8 %copy-start.10 = (bf16[128,512]{1,0:T(8,128)(2,1)}, bf16[128,512]{1,0:T(8,128)(2,1)S(1)}, u32[]{:S(2)}) copy-start(bf16[128,512]{1,0:T(8,128)(2,1)S(1)} %collective-permute-done.7.refs_0_) | copy-start | bytes 393220
  25.3 5.3 %collective-permute-start.9 = (bf16[128,512]{1,0:T(8,128)(2,1)S(1)}, bf16[128,512]{1,0:T(8,128)(2,1)}, u32[]{:S(2)}, u32[]{:S(2)}) collective-permute-start(bf16[128,512]{1,0:T(8,128)(2,1)S(1)} %get-tuple-element.65), channel_id=1, source_target_pairs={{0,2},{1,3},{2,0},{3,1},{4,6},{5,7},{6,4},{7,5},{8,10},{9,11},{10,... | collective-permute-start | bytes 393224 | tf_op jit(solution)/shard_map/ppermute | solution.py:22
  30.6 21.5 %collective-permute-start.8 = (bf16[128,512]{1,0:T(8,128)(2,1)S(1)}, bf16[128,512]{1,0:T(8,128)(2,1)}, u32[]{:S(2)}, u32[]{:S(2)}) collective-permute-start(bf16[128,512]{1,0:T(8,128)(2,1)S(1)} %collective-permute-done.7.refs_0_), channel_id=1, source_target_pairs={{0,1},{1,0},{2,3},{3,2},{4,5},{5,4},{6,7},{7,6},{8,9},{9,8},{10,11... | collective-permute-start | bytes 393224 | tf_op jit(solution)/shard_map/ppermute | solution.py:22
  30.6 25.2 %collective-permute-start.10 = (bf16[128,512]{1,0:T(8,128)(2,1)}, bf16[128,512]{1,0:T(8,128)(2,1)}, u32[]{:S(2)}, u32[]{:S(2)}) collective-permute-start(bf16[128,512]{1,0:T(8,128)(2,1)} %collective-permute-done.9.refs_0_), channel_id=1, source_target_pairs={{0,1},{1,0},{2,3},{3,2},{4,5},{5,4},{6,7},{7,6},{8,9},{9,8},{10,11... | collective-permute-start | bytes 393224 | tf_op jit(solution)/shard_map/ppermute | solution.py:22
  31.1 1.6 %copy-start.1 = (bf16[2048,512]{1,0:T(8,128)(2,1)S(1)}, bf16[2048,512]{1,0:T(8,128)(2,1)}, u32[]{:S(2)}) copy-start(bf16[2048,512]{1,0:T(8,128)(2,1)} %refs_3_.11) | copy-start | bytes 6291460
  32.7 1.6 %copy-start.3 = (bf16[2048,512]{1,0:T(8,128)(2,1)S(1)}, bf16[2048,512]{1,0:T(8,128)(2,1)}, u32[]{:S(2)}) copy-start(bf16[2048,512]{1,0:T(8,128)(2,1)} %refs_2_.21) | copy-start | bytes 6291460
  34.3 1.2 %copy-start.8 = (bf16[1024,512]{1,0:T(8,128)(2,1)S(1)}, bf16[1024,512]{1,0:T(8,128)(2,1)}, u32[]{:S(2)}) copy-start(bf16[1024,512]{1,0:T(8,128)(2,1)} %tokens.3) | copy-start | bytes 3145732
  35.5 5.3 %copy-start.2 = (bf16[2048,512]{1,0:T(8,128)(2,1)S(1)}, bf16[2048,512]{1,0:T(8,128)(2,1)}, u32[]{:S(2)}) copy-start(bf16[2048,512]{1,0:T(8,128)(2,1)} %refs_3_.11) | copy-start | bytes 6291460
  39.5 1.4 %copy-start.5 = (f32[1024,512]{1,0:T(8,128)}, f32[1024,512]{1,0:T(8,128)S(1)}, u32[]{:S(2)}) copy-start(f32[1024,512]{1,0:T(8,128)S(1)} %get-tuple-element.44.refs_3_) | copy-start | bytes 6291460
  43.7 0.7 copy-start.20
  44.4 0.7 copy-start.22
  47.9 0.7 copy-start.16
  48.6 2.8 %copy-start.18 = (bf16[256,512]{1,0:T(8,128)(2,1)}, bf16[256,512]{1,0:T(8,128)(2,1)S(1)}, u32[]{:S(2)}) copy-start(bf16[256,512]{1,0:T(8,128)(2,1)S(1)} %get-tuple-element.53.refs_5_) | copy-start | bytes 786436
  51.4 0.7 copy-start.14
  52.1 2.4 %copy-start.12 = (bf16[256,512]{1,0:T(8,128)(2,1)}, bf16[256,512]{1,0:T(8,128)(2,1)S(1)}, u32[]{:S(2)}) copy-start(bf16[256,512]{1,0:T(8,128)(2,1)S(1)} %get-tuple-element.57.refs_4_) | copy-start | bytes 786436
  54.6 0.6 copy-start.28
  55.2 0.7 copy-start.30
  55.9 10.6 %copy-start.33 = (f32[4,16]{1,0:T(4,128)S(1)}, f32[4,16]{1,0:T(4,128)}, u32[]{:S(2)}) copy-start(f32[4,16]{1,0:T(4,128)} %table.1) | copy-start | bytes 772
  55.9 10.8 %copy-start.9 = (s32[6,1024]{1,0:T(8,128)S(1)}, s32[6,1024]{1,0:T(8,128)}, u32[]{:S(2)}) copy-start(s32[6,1024]{1,0:T(8,128)} %refs_6_.9) | copy-start | bytes 73732
  57.6 6.2 %copy-start.24 = (bf16[128,512]{1,0:T(8,128)(2,1)}, bf16[128,512]{1,0:T(8,128)(2,1)S(1)}, u32[]{:S(2)}) copy-start(bf16[128,512]{1,0:T(8,128)(2,1)S(1)} %get-tuple-element.67.refs_4_) | copy-start | bytes 393220
  57.6 6.2 %copy-start.26 = (bf16[128,512]{1,0:T(8,128)(2,1)}, bf16[128,512]{1,0:T(8,128)(2,1)S(1)}, u32[]{:S(2)}) copy-start(bf16[128,512]{1,0:T(8,128)(2,1)S(1)} %get-tuple-element.68.refs_5_) | copy-start | bytes 393220
  57.6 5.5 %collective-permute-start.11 = (bf16[4,128,128]{2,1,0:T(8,128)(2,1)S(1)}, bf16[4,128,128]{2,1,0:T(8,128)(2,1)S(1)}, u32[]{:S(2)}, u32[]{:S(2)}) collective-permute-start(bf16[4,128,128]{2,1,0:T(8,128)(2,1)S(1)} %get-tuple-element.80), channel_id=1, source_target_pairs={{0,4},{4,0},{8,12},{12,8},{1,5},{5,1},{9,13},{13,9},{2,6},{6,2},{1... | collective-permute-start | bytes 393224 | tf_op jit(solution)/shard_map/ppermute | solution.py:22
  63.9 20.1 %collective-permute-start.12 = (bf16[4,128,128]{2,1,0:T(8,128)(2,1)S(1)}, bf16[4,128,128]{2,1,0:T(8,128)(2,1)S(1)}, u32[]{:S(2)}, u32[]{:S(2)}) collective-permute-start(bf16[4,128,128]{2,1,0:T(8,128)(2,1)S(1)} %get-tuple-element.82), channel_id=1, source_target_pairs={{0,8},{4,12},{8,0},{12,4},{1,9},{5,13},{9,1},{13,5},{2,10},{6,14},... | collective-permute-start | bytes 393224 | tf_op jit(solution)/shard_map/ppermute | solution.py:22
  66.7 1.6 %copy-start.4 = (bf16[2048,512]{1,0:T(8,128)(2,1)S(1)}, bf16[2048,512]{1,0:T(8,128)(2,1)}, u32[]{:S(2)}) copy-start(bf16[2048,512]{1,0:T(8,128)(2,1)} %refs_2_.21) | copy-start | bytes 6291460
  68.3 1.6 %copy-start.6 = (f32[1024,512]{1,0:T(8,128)S(1)}, f32[1024,512]{1,0:T(8,128)}, u32[]{:S(2)}) copy-start(f32[1024,512]{1,0:T(8,128)} %copy-done.5) | copy-start | bytes 6291460
  69.9 0.9 %copy-start.21 = (bf16[256,512]{1,0:T(8,128)(2,1)S(1)}, bf16[256,512]{1,0:T(8,128)(2,1)}, u32[]{:S(2)}) copy-start(bf16[256,512]{1,0:T(8,128)(2,1)} %copy-done.20) | copy-start | bytes 786436
  70.8 0.9 %copy-start.23 = (bf16[256,512]{1,0:T(8,128)(2,1)S(1)}, bf16[256,512]{1,0:T(8,128)(2,1)}, u32[]{:S(2)}) copy-start(bf16[256,512]{1,0:T(8,128)(2,1)} %copy-done.22) | copy-start | bytes 786436
  71.8 2.8 %copy-start.17 = (bf16[256,512]{1,0:T(8,128)(2,1)S(1)}, bf16[256,512]{1,0:T(8,128)(2,1)}, u32[]{:S(2)}) copy-start(bf16[256,512]{1,0:T(8,128)(2,1)} %copy-done.16) | copy-start | bytes 786436
  71.8 2.8 %copy-start.19 = (bf16[256,512]{1,0:T(8,128)(2,1)S(1)}, bf16[256,512]{1,0:T(8,128)(2,1)}, u32[]{:S(2)}) copy-start(bf16[256,512]{1,0:T(8,128)(2,1)} %copy-done.18) | copy-start | bytes 786436
  74.6 2.6 %copy-start.13 = (bf16[256,512]{1,0:T(8,128)(2,1)S(1)}, bf16[256,512]{1,0:T(8,128)(2,1)}, u32[]{:S(2)}) copy-start(bf16[256,512]{1,0:T(8,128)(2,1)} %copy-done.12) | copy-start | bytes 786436
  74.6 2.6 %copy-start.15 = (bf16[256,512]{1,0:T(8,128)(2,1)S(1)}, bf16[256,512]{1,0:T(8,128)(2,1)}, u32[]{:S(2)}) copy-start(bf16[256,512]{1,0:T(8,128)(2,1)} %copy-done.14) | copy-start | bytes 786436
  77.2 2.5 %copy-start.11 = (bf16[128,512]{1,0:T(8,128)(2,1)S(1)}, bf16[128,512]{1,0:T(8,128)(2,1)}, u32[]{:S(2)}) copy-start(bf16[128,512]{1,0:T(8,128)(2,1)} %copy-done.10) | copy-start | bytes 393220
  77.2 2.5 %copy-start.29 = (bf16[128,512]{1,0:T(8,128)(2,1)S(1)}, bf16[128,512]{1,0:T(8,128)(2,1)}, u32[]{:S(2)}) copy-start(bf16[128,512]{1,0:T(8,128)(2,1)} %copy-done.28) | copy-start | bytes 393220
  77.2 2.5 %copy-start.31 = (bf16[128,512]{1,0:T(8,128)(2,1)S(1)}, bf16[128,512]{1,0:T(8,128)(2,1)}, u32[]{:S(2)}) copy-start(bf16[128,512]{1,0:T(8,128)(2,1)} %copy-done.30) | copy-start | bytes 393220
  79.7 2.1 %copy-start.25 = (bf16[128,512]{1,0:T(8,128)(2,1)S(1)}, bf16[128,512]{1,0:T(8,128)(2,1)}, u32[]{:S(2)}) copy-start(bf16[128,512]{1,0:T(8,128)(2,1)} %copy-done.24) | copy-start | bytes 393220
  79.7 2.1 %copy-start.27 = (bf16[128,512]{1,0:T(8,128)(2,1)S(1)}, bf16[128,512]{1,0:T(8,128)(2,1)}, u32[]{:S(2)}) copy-start(bf16[128,512]{1,0:T(8,128)(2,1)} %copy-done.26) | copy-start | bytes 393220
  81.8 2.1 %copy-start.32 = (f32[512]{0:T(512)S(1)}, f32[512]{0:T(512)}, u32[]{:S(2)}) copy-start(f32[512]{0:T(512)} %param.13) | copy-start | bytes 6148
where the time goes:
time: 86.1 us; the launch traced here: 85.6 us
  Pallas kernels  31.5 us (37%)
  waiting for transfers between devices  25.6 us (30%)
  local copies, waits for them, and re-layouts  16.4 us (19%)
  starting transfers between devices  11.8 us (14%)
    pallas_call x16, Pallas kernels, call(): pl.pallas_call(kernel, out_shape=[jax.ShapeDtypeStruct(*out) for out in o...  31.5 us
    ppermute x13, waiting for transfers between devices, swap(): return lax.ppermute(block, axis, route)  25.6 us
    unnamed x68, local copies, waits for them, and re-layouts  16.4 us
    ppermute x13, starting transfers between devices, swap(): return lax.ppermute(block, axis, route)  11.8 us
  transfers between devices with their start and end apart: 13, of which 6 were waited for; matrix products, arithmetic and copies ran while one was open for 0% of the time, Pallas kernels for 32%

commit v1 on v0

--- a/solution.py
+++ b/solution.py
@@ -13,7 +13,6 @@
 F32 = jnp.float32
 BF16 = jnp.bfloat16
 VMEM = pl.BlockSpec(memory_space=pltpu.VMEM)
-SMEM = pl.BlockSpec(memory_space=pltpu.SMEM)
 ANY = pl.BlockSpec(memory_space=pl.ANY)
 
 
@@ -26,10 +25,15 @@
     return lax.dot_general(a, b, (dims, ((), ())), preferred_element_type=F32)
 
 
+def keep(array):
+    return pltpu.with_memory_space_constraint(array, pltpu.VMEM)
+
+
 def call(kernel, outs, in_specs, args, out_specs=None, scratch=(), limit=8):
+    kept = [pltpu.VMEM(*out) for out in outs]
     return pl.pallas_call(
         kernel,
-        out_shape=[jax.ShapeDtypeStruct(*out) for out in outs],
+        out_shape=kept if out_specs is None else [jax.ShapeDtypeStruct(*out) for out in outs],
         in_specs=in_specs,
         out_specs=out_specs or [VMEM] * len(outs),
         scratch_shapes=scratch,
@@ -58,7 +62,8 @@
         copy.wait()
 
 
-def early_kernel(n_near, tile, me, *refs):
+def early_kernel(n_near, tile, *refs):
+    me = lax.axis_index("head")
     pieces = refs[:n_near]
     weights = refs[n_near : n_near + 3]
     sums = refs[n_near + 3 :]
@@ -69,7 +74,7 @@
         for weight, total in zip(weights, sums):
             acc = None
             for offset, piece in enumerate(pieces):
-                part = dot(piece[at, :], weight_rows(me[0], weight, offset, depth))
+                part = dot(piece[at, :], weight_rows(me, weight, offset, depth))
                 acc = part if acc is None else acc + part
             total[at, :] = acc
         return carry
@@ -77,7 +82,8 @@
     lax.fori_loop(0, rows // tile, step, 0)
 
 
-def late_sum(me, base, pieces, weight, early, lo, rows):
+def late_sum(base, pieces, weight, early, lo, rows):
+    me = lax.axis_index("head")
     depth = pieces[0].shape[1]
     acc = early[lo : lo + rows, :]
     for offset, piece in enumerate(pieces):
@@ -85,16 +91,16 @@
     return acc
 
 
-def kv_kernel(base, lo, heads, me, *refs):
+def kv_kernel(base, lo, heads, *refs):
     pieces = refs[:base]
     k_weight, v_weight, k_early, v_early = refs[base : base + 4]
     state_in = refs[base + 4] if lo else None
     keys, values, state, state_low = refs[-4:]
     rows, width = keys.shape
     size = width // heads
-    raw_v = late_sum(me[0], base, pieces, v_weight, v_early, lo, rows).astype(BF16)
+    raw_v = late_sum(base, pieces, v_weight, v_early, lo, rows).astype(BF16)
     values[...] = raw_v
-    raw_k = late_sum(me[0], base, pieces, k_weight, k_early, lo, rows)
+    raw_k = late_sum(base, pieces, k_weight, k_early, lo, rows)
     for head in range(heads):
         cols = slice(head * size, (head + 1) * size)
         key = unit_rows(raw_k[:, cols])
@@ -139,7 +145,7 @@
     return weigh(picked(0)), weigh(rest), far
 
 
-def query_kernel(base, lo, heads, depth, me, block, *refs):
+def query_kernel(base, lo, heads, depth, *refs):
     pieces = refs[:base]
     q_weight, q_early, keys, values, index, table = refs[base : base + 6]
     state_in = refs[base + 6] if lo else None
@@ -147,8 +153,8 @@
     scaled = refs[-depth:]
     rows, width = keys.shape
     size = width // heads
-    own, rest, far = level_weights(depth, block[0], index[:, lo : lo + rows], table)
-    raw_q = late_sum(me[0], base, pieces, q_weight, q_early, lo, rows)
+    own, rest, far = level_weights(depth, lax.axis_index("seq"), index[:, lo : lo + rows], table)
+    raw_q = late_sum(base, pieces, q_weight, q_early, lo, rows)
     causal = lax.broadcasted_iota(jnp.int32, (rows, rows), 0) >= lax.broadcasted_iota(jnp.int32, (rows, rows), 1)
     for head in range(heads):
         cols = slice(head * size, (head + 1) * size)
@@ -212,14 +218,14 @@
     size = width // heads
     base = lax.axis_size("head") // 2
     depth = lax.axis_size("seq").bit_length() - 1
-    me = lax.axis_index("head").astype(jnp.int32).reshape(1)
-    block = lax.axis_index("seq").astype(jnp.int32).reshape(1)
 
     unit = row_count // sum(CHUNKS)
     edges = [0]
     for share in CHUNKS:
         edges.append(edges[-1] + share * unit)
     spans = list(zip(edges[:-1], edges[1:]))
+
+    q_weight, k_weight, v_weight = (keep(weight) for weight in (q_weight, k_weight, v_weight))
 
     cuts = []
     for group in (spans[:1], spans[1:]):
@@ -237,8 +243,8 @@
     early = call(
         functools.partial(early_kernel, base, row_count // 4),
         [(big, F32)] * 3,
-        [SMEM] + [VMEM] * (base + 3),
-        (me, *near, q_weight, k_weight, v_weight),
+        [VMEM] * (base + 3),
+        (*near, q_weight, k_weight, v_weight),
     )
     table = call(table_kernel, [((2 * quant, width), BF16)], [VMEM], (level_table,))[0]
 
@@ -249,19 +255,19 @@
         rows = hi - lo
         pieces = hop(far[i], base)
         before = state
-        args = (me, *pieces, k_weight, v_weight, early[1], early[2], *before)
+        args = (*pieces, k_weight, v_weight, early[1], early[2], *before)
         keys, values, total, low = call(
             functools.partial(kv_kernel, base, lo, heads),
             [((rows, width), BF16)] * 2 + [((heads, size, size), F32), ((heads, size, size), BF16)],
-            [SMEM] + [VMEM] * (len(args) - 1),
+            [VMEM] * len(args),
             args,
         )
         state = [total]
-        args = (me, block, *pieces, q_weight, early[0], keys, values, level_index, table, *before)
+        args = (*pieces, q_weight, early[0], keys, values, level_index, table, *before)
         outs = call(
             functools.partial(query_kernel, base, lo, heads, depth),
             [((rows, width), F32)] + [((rows, width), BF16)] * depth,
-            [SMEM, SMEM] + [VMEM] * (len(args) - 2),
+            [VMEM] * len(args),
             args,
         )
         parts.append(outs[0])

time: 86.1 us -> 63.3 us (0.74)
  local copies, waits for them, and re-layouts: 16.4 us -> 4.57 us
  Pallas kernels: 31.5 us -> 21.2 us
    unnamed x68 -> x18, local copies, waits for them, and re-layouts: 16.4 us -> 4.57 us
    pallas_call x16, Pallas kernels: 31.5 us -> 21.2 us  [call(): pl.pallas_call(kernel, out_shape=kept if out_specs is None else [jax.Shap...]
  transfers between devices with their start and end apart: 13 -> 13, of which waited for: 6 -> 6; matrix products, arithmetic and copies ran while one was open for 0% -> 0% of each run, Pallas kernels for 32% -> 29%
where the time goes in v1:
time: 63.3 us; the launch traced here: 63.2 us
  waiting for transfers between devices  25.5 us (40%)
  Pallas kernels  21.2 us (33%)
  starting transfers between devices  11.8 us (19%)
  local copies, waits for them, and re-layouts  4.57 us (7%)
    ppermute x13, waiting for transfers between devices, swap(): return lax.ppermute(block, axis, route)  25.5 us
    pallas_call x16, Pallas kernels, call(): pl.pallas_call(kernel, out_shape=kept if out_specs is None else [jax.Shap...  21.2 us
    ppermute x13, starting transfers between devices, swap(): return lax.ppermute(block, axis, route)  11.8 us
    unnamed x18, local copies, waits for them, and re-layouts  4.57 us
  transfers between devices with their start and end apart: 13, of which 6 were waited for; matrix products, arithmetic and copies ran while one was open for 0% of the time, Pallas kernels for 29%

profile of v1, /device:TPU:0, one launch (start us, length us, event | category | flops | bytes accessed | tf_op | source)
XLA Modules:
  0.0 63.2 jit_solution(10647243969745567486)
XLA Ops:
  0.0 0.5 collective-permute-start.2
  0.5 1.4 %copy-done.5 = bf16[1024,512]{1,0:T(8,128)(2,1)S(1)} copy-done((bf16[1024,512]{1,0:T(8,128)(2,1)S(1)}, bf16[1024,512]{1,0:T(8,128)(2,1)}, u32[]{:S(2)}) %copy-start.5) | copy-done | bytes 1048600
  1.9 2.6 %collective-permute-start = (bf16[256,512]{1,0:T(8,128)(2,1)S(1)}, bf16[256,512]{1,0:T(8,128)(2,1)S(1)}, u32[]{:S(2)}, u32[]{:S(2)}) collective-permute-start(bf16[256,512]{1,0:T(8,128)(2,1)S(1)} %shard_map.73), channel_id=1, source_target_pairs={{0,2},{1,3},{2,0},{3,1},{4,6},{5,7},{6,4},{7,5},{8,10},{9,11},{10,... | collective-permute-start | bytes 786440 | tf_op jit(solution)/shard_map/ppermute | solution.py:21
  4.4 0.4 shard_map.78
  4.9 0.1 collective-permute-start.3
  5.0 2.0 %collective-permute-start.5 = (bf16[256,512]{1,0:T(8,128)(2,1)S(1)}, bf16[256,512]{1,0:T(8,128)(2,1)S(1)}, u32[]{:S(2)}, u32[]{:S(2)}) collective-permute-start(bf16[256,512]{1,0:T(8,128)(2,1)S(1)} %get-tuple-element.55), channel_id=1, source_target_pairs={{0,2},{1,3},{2,0},{3,1},{4,6},{5,7},{6,4},{7,5},{8,10},{9,11},{10,... | collective-permute-start | bytes 786440 | tf_op jit(solution)/shard_map/ppermute | solution.py:21
  7.0 0.1 collective-permute-start.7
  7.0 4.6 %collective-permute-done.refs_0_ = bf16[256,512]{1,0:T(8,128)(2,1)S(1)} collective-permute-done((bf16[256,512]{1,0:T(8,128)(2,1)S(1)}, bf16[256,512]{1,0:T(8,128)(2,1)S(1)}, u32[]{:S(2)}, u32[]{:S(2)}) %collective-permute-start) | collective-permute-done | bytes 262176 | tf_op jit(solution)/shard_map/ppermute | solution.py:21
  11.6 0.0 collective-permute-start.1
  11.6 5.6 %collective-permute-done.3.refs_0_ = bf16[256,512]{1,0:T(8,128)(2,1)S(1)} collective-permute-done((bf16[256,512]{1,0:T(8,128)(2,1)S(1)}, bf16[256,512]{1,0:T(8,128)(2,1)S(1)}, u32[]{:S(2)}, u32[]{:S(2)}) %collective-permute-start.3) | collective-permute-done | bytes 262176 | tf_op jit(solution)/shard_map/ppermute | solution.py:21
  17.2 0.0 collective-permute-start.4
  17.2 5.6 %collective-permute-done.5.refs_0_ = bf16[256,512]{1,0:T(8,128)(2,1)S(1)} collective-permute-done((bf16[256,512]{1,0:T(8,128)(2,1)S(1)}, bf16[256,512]{1,0:T(8,128)(2,1)S(1)}, u32[]{:S(2)}, u32[]{:S(2)}) %collective-permute-start.5) | collective-permute-done | bytes 262176 | tf_op jit(solution)/shard_map/ppermute | solution.py:21
  22.8 0.0 collective-permute-start.6
  22.8 2.5 %collective-permute-done.7.refs_0_ = bf16[128,512]{1,0:T(8,128)(2,1)S(1)} collective-permute-done((bf16[128,512]{1,0:T(8,128)(2,1)S(1)}, bf16[128,512]{1,0:T(8,128)(2,1)S(1)}, u32[]{:S(2)}, u32[]{:S(2)}) %collective-permute-start.7) | collective-permute-done | bytes 131104 | tf_op jit(solution)/shard_map/ppermute | solution.py:21
  25.3 1.7 %collective-permute-start.9 = (bf16[128,512]{1,0:T(8,128)(2,1)S(1)}, bf16[128,512]{1,0:T(8,128)(2,1)S(1)}, u32[]{:S(2)}, u32[]{:S(2)}) collective-permute-start(bf16[128,512]{1,0:T(8,128)(2,1)S(1)} %get-tuple-element.65), channel_id=1, source_target_pairs={{0,2},{1,3},{2,0},{3,1},{4,6},{5,7},{6,4},{7,5},{8,10},{9,11},{10,... | collective-permute-start | bytes 393224 | tf_op jit(solution)/shard_map/ppermute | solution.py:21
  27.1 3.4 %collective-permute-done.9.refs_0_ = bf16[128,512]{1,0:T(8,128)(2,1)S(1)} collective-permute-done((bf16[128,512]{1,0:T(8,128)(2,1)S(1)}, bf16[128,512]{1,0:T(8,128)(2,1)S(1)}, u32[]{:S(2)}, u32[]{:S(2)}) %collective-permute-start.9) | collective-permute-done | bytes 131104 | tf_op jit(solution)/shard_map/ppermute | solution.py:21
  30.5 0.0 collective-permute-start.8
  30.5 0.0 collective-permute-done.2.refs_1_
  30.5 0.5 collective-permute-start.10
  31.0 0.0 copy-done
  31.0 1.6 %copy-done.1 = bf16[2048,512]{1,0:T(8,128)(2,1)S(1)} copy-done((bf16[2048,512]{1,0:T(8,128)(2,1)S(1)}, bf16[2048,512]{1,0:T(8,128)(2,1)}, u32[]{:S(2)}) %copy-start.1) | copy-done | bytes 2097176
  32.6 1.6 %copy-done.3 = bf16[2048,512]{1,0:T(8,128)(2,1)S(1)} copy-done((bf16[2048,512]{1,0:T(8,128)(2,1)S(1)}, bf16[2048,512]{1,0:T(8,128)(2,1)}, u32[]{:S(2)}) %copy-start.3) | copy-done | bytes 2097176
  34.2 3.9 %shard_map.74 = (f32[1024,512]{1,0:T(8,128)S(1)}, f32[1024,512]{1,0:T(8,128)S(1)}, f32[1024,512]{1,0:T(8,128)S(1)}) custom-call(bf16[1024,512]{1,0:T(8,128)(2,1)S(1)} %copy-done.5, bf16[1024,512]{1,0:T(8,128)(2,1)S(1)} %collective-permute-done.2.refs_1_, bf16[2048,512]{1,0:T(8,128)(2,1)S(1)} %copy-done.3, bf16[2048,512]{1,0:T(8,128)(2,1)S(1)} %copy-done, ...), custom_call_target="tpu_custom_call" | custom-call | tf_op jit(solution)/shard_map/pallas_call | solution.py:34
  38.1 0.0 collective-permute-done.1.refs_1_
  38.1 0.0 copy-done.2
  38.1 1.8 %shard_map.75 = (bf16[256,512]{1,0:T(8,128)(2,1)S(1)}, bf16[256,512]{1,0:T(8,128)(2,1)S(1)}, f32[4,128,128]{2,1,0:T(8,128)S(1)}, bf16[4,128,128]{2,1,0:T(8,128)(2,1)}) custom-call(bf16[256,512]{1,0:T(8,128)(2,1)S(1)} %collective-permute-done.refs_0_, bf16[256,512]{1,0:T(8,128)(2,1)S(1)} %collective-permute-done.1.refs_1_, bf16[2048,512]{1,0:T(8,128)(2,1)S(1)} %copy-done, ...), custom_call_target="tpu_custom_call" | custom-call | tf_op jit(solution)/shard_map/pallas_call | solution.py:34
  39.9 0.0 collective-permute-done.4.refs_1_
  39.9 1.8 %shard_map.79 = (bf16[256,512]{1,0:T(8,128)(2,1)S(1)}, bf16[256,512]{1,0:T(8,128)(2,1)S(1)}, f32[4,128,128]{2,1,0:T(8,128)S(1)}, bf16[4,128,128]{2,1,0:T(8,128)(2,1)}) custom-call(bf16[256,512]{1,0:T(8,128)(2,1)S(1)} %collective-permute-done.3.refs_0_, bf16[256,512]{1,0:T(8,128)(2,1)S(1)} %collective-permute-done.4.refs_1_, bf16[2048,512]{1,0:T(8,128)(2,1)S(1)} %copy-done, ...), custom_call_target="tpu_custom_call" | custom-call | tf_op jit(solution)/shard_map/pallas_call | solution.py:34
  41.7 0.0 collective-permute-done.6.refs_1_
  41.7 1.8 %shard_map.81 = (bf16[256,512]{1,0:T(8,128)(2,1)S(1)}, bf16[256,512]{1,0:T(8,128)(2,1)S(1)}, f32[4,128,128]{2,1,0:T(8,128)S(1)}, bf16[4,128,128]{2,1,0:T(8,128)(2,1)}) custom-call(bf16[256,512]{1,0:T(8,128)(2,1)S(1)} %collective-permute-done.5.refs_0_, bf16[256,512]{1,0:T(8,128)(2,1)S(1)} %collective-permute-done.6.refs_1_, bf16[2048,512]{1,0:T(8,128)(2,1)S(1)} %copy-done, ...), custom_call_target="tpu_custom_call" | custom-call | tf_op jit(solution)/shard_map/pallas_call | solution.py:34
  43.5 0.0 collective-permute-done.8.refs_1_
  43.5 1.4 %shard_map.83 = (bf16[128,512]{1,0:T(8,128)(2,1)S(1)}, bf16[128,512]{1,0:T(8,128)(2,1)S(1)}, f32[4,128,128]{2,1,0:T(8,128)S(1)}, bf16[4,128,128]{2,1,0:T(8,128)(2,1)}) custom-call(bf16[128,512]{1,0:T(8,128)(2,1)S(1)} %collective-permute-done.7.refs_0_, bf16[128,512]{1,0:T(8,128)(2,1)S(1)} %collective-permute-done.8.refs_1_, bf16[2048,512]{1,0:T(8,128)(2,1)S(1)} %copy-done, ...), custom_call_target="tpu_custom_call" | custom-call | tf_op jit(solution)/shard_map/pallas_call | solution.py:34
  44.9 0.0 collective-permute-done.10.refs_1_
  44.9 0.8 %shard_map.85 = (bf16[128,512]{1,0:T(8,128)(2,1)S(1)}, bf16[128,512]{1,0:T(8,128)(2,1)S(1)}, f32[4,128,128]{2,1,0:T(8,128)S(1)}, bf16[4,128,128]{2,1,0:T(8,128)(2,1)S(1)}) custom-call(bf16[128,512]{1,0:T(8,128)(2,1)S(1)} %collective-permute-done.9.refs_0_, bf16[128,512]{1,0:T(8,128)(2,1)S(1)} %collective-permute-done.10.refs_1_, ...), custom_call_target="tpu_custom_call" | custom-call | tf_op jit(solution)/shard_map/pallas_call | solution.py:34
  45.7 1.7 %collective-permute-start.11 = (bf16[4,128,128]{2,1,0:T(8,128)(2,1)S(1)}, bf16[4,128,128]{2,1,0:T(8,128)(2,1)S(1)}, u32[]{:S(2)}, u32[]{:S(2)}) collective-permute-start(bf16[4,128,128]{2,1,0:T(8,128)(2,1)S(1)} %get-tuple-element.80), channel_id=1, source_target_pairs={{0,4},{4,0},{8,12},{12,8},{1,5},{5,1},{9,13},{13,9},{2,6},{6,2},{1... | collective-permute-start | bytes 393224 | tf_op jit(solution)/shard_map/ppermute | solution.py:21
  47.4 3.8 %collective-permute-done.11.partner.refs_15_ = bf16[4,128,128]{2,1,0:T(8,128)(2,1)S(1)} collective-permute-done((bf16[4,128,128]{2,1,0:T(8,128)(2,1)S(1)}, bf16[4,128,128]{2,1,0:T(8,128)(2,1)S(1)}, u32[]{:S(2)}, u32[]{:S(2)}) %collective-permute-start.11) | collective-permute-done | bytes 131104 | tf_op jit(solution)/shard_map/ppermute | solution.py:21
  51.2 0.7 %shard_map.87 = (f32[4,128,128]{2,1,0:T(8,128)}, bf16[4,128,128]{2,1,0:T(8,128)(2,1)S(1)}) custom-call(f32[4,128,128]{2,1,0:T(8,128)S(1)} %get-tuple-element.81.total, bf16[4,128,128]{2,1,0:T(8,128)(2,1)S(1)} %collective-permute-done.11.partner.refs_15_), custom_call_target="tpu_custom_call" | custom-call | tf_op jit(solution)/shard_map/pallas_call | solution.py:34
  51.9 2.6 %collective-permute-start.12 = (bf16[4,128,128]{2,1,0:T(8,128)(2,1)S(1)}, bf16[4,128,128]{2,1,0:T(8,128)(2,1)S(1)}, u32[]{:S(2)}, u32[]{:S(2)}) collective-permute-start(bf16[4,128,128]{2,1,0:T(8,128)(2,1)S(1)} %get-tuple-element.82), channel_id=1, source_target_pairs={{0,8},{4,12},{8,0},{12,4},{1,9},{5,13},{9,1},{13,5},{2,10},{6,14},... | collective-permute-start | bytes 393224 | tf_op jit(solution)/shard_map/ppermute | solution.py:21
  54.5 0.0 copy-done.8
  54.5 0.2 shard_map.76.refs_7_
  54.7 1.7 %shard_map.77 = (f32[256,512]{1,0:T(8,128)S(1)}, bf16[256,512]{1,0:T(8,128)(2,1)S(1)}, bf16[256,512]{1,0:T(8,128)(2,1)S(1)}) custom-call(bf16[256,512]{1,0:T(8,128)(2,1)S(1)} %collective-permute-done.refs_0_, bf16[256,512]{1,0:T(8,128)(2,1)S(1)} %collective-permute-done.1.refs_1_, bf16[2048,512]{1,0:T(8,128)(2,1)S(1)} %copy-done.4, ...), custom_call_target="tpu_custom_call" | custom-call | tf_op jit(solution)/shard_map/pallas_call | solution.py:34
  56.4 1.4 %shard_map.80 = (f32[256,512]{1,0:T(8,128)S(1)}, bf16[256,512]{1,0:T(8,128)(2,1)S(1)}, bf16[256,512]{1,0:T(8,128)(2,1)S(1)}) custom-call(bf16[256,512]{1,0:T(8,128)(2,1)S(1)} %collective-permute-done.3.refs_0_, bf16[256,512]{1,0:T(8,128)(2,1)S(1)} %collective-permute-done.4.refs_1_, bf16[2048,512]{1,0:T(8,128)(2,1)S(1)} %copy-done.4, ...), custom_call_target="tpu_custom_call" | custom-call | tf_op jit(solution)/shard_map/pallas_call | solution.py:34
  57.8 1.4 %shard_map.82 = (f32[256,512]{1,0:T(8,128)S(1)}, bf16[256,512]{1,0:T(8,128)(2,1)S(1)}, bf16[256,512]{1,0:T(8,128)(2,1)S(1)}) custom-call(bf16[256,512]{1,0:T(8,128)(2,1)S(1)} %collective-permute-done.5.refs_0_, bf16[256,512]{1,0:T(8,128)(2,1)S(1)} %collective-permute-done.6.refs_1_, bf16[2048,512]{1,0:T(8,128)(2,1)S(1)} %copy-done.4, ...), custom_call_target="tpu_custom_call" | custom-call | tf_op jit(solution)/shard_map/pallas_call | solution.py:34
  59.3 1.1 %shard_map.84 = (f32[128,512]{1,0:T(8,128)S(1)}, bf16[128,512]{1,0:T(8,128)(2,1)S(1)}, bf16[128,512]{1,0:T(8,128)(2,1)S(1)}) custom-call(bf16[128,512]{1,0:T(8,128)(2,1)S(1)} %collective-permute-done.7.refs_0_, bf16[128,512]{1,0:T(8,128)(2,1)S(1)} %collective-permute-done.8.refs_1_, bf16[2048,512]{1,0:T(8,128)(2,1)S(1)} %copy-done.4, ...), custom_call_target="tpu_custom_call" | custom-call | tf_op jit(solution)/shard_map/pallas_call | solution.py:34
  60.4 0.0 copy-start.7
  60.4 1.1 %shard_map.86 = (f32[128,512]{1,0:T(8,128)S(1)}, bf16[128,512]{1,0:T(8,128)(2,1)S(1)}, bf16[128,512]{1,0:T(8,128)(2,1)S(1)}) custom-call(bf16[128,512]{1,0:T(8,128)(2,1)S(1)} %collective-permute-done.9.refs_0_, bf16[128,512]{1,0:T(8,128)(2,1)S(1)} %collective-permute-done.10.refs_1_, bf16[2048,512]{1,0:T(8,128)(2,1)S(1)} %copy-done.4, ...), custom_call_target="tpu_custom_call" | custom-call | tf_op jit(solution)/shard_map/pallas_call | solution.py:34
  61.6 0.0 collective-permute-done.12.refs_16_
  61.6 1.6 %shard_map.88 = bf16[1024,512]{1,0:T(8,128)(2,1)} custom-call(f32[256,512]{1,0:T(8,128)S(1)} %get-tuple-element.49.refs_0_, f32[256,512]{1,0:T(8,128)S(1)} %get-tuple-element.54.refs_1_, f32[256,512]{1,0:T(8,128)S(1)} %get-tuple-element.59.refs_2_, f32[128,512]{1,0:T(8,128)S(1)} %get-tuple-element.64.refs_3_, f32[128,512]{1,0:T(8,128)S(1)} %get-tuple-element.69.refs_4_, ...), custom_call_target="tpu_custom_call" | custom-call | tf_op jit(solution)/shard_map/pallas_call | solution.py:34
  (12 shorter events, 0.0 us)
Async XLA Ops:
  0.0 31.0 %copy-start = (bf16[2048,512]{1,0:T(8,128)(2,1)S(1)}, bf16[2048,512]{1,0:T(8,128)(2,1)}, u32[]{:S(2)}) copy-start(bf16[2048,512]{1,0:T(8,128)(2,1)} %refs_2_.20) | copy-start | bytes 6291460
  0.0 30.5 %collective-permute-start.2 = (bf16[1024,512]{1,0:T(8,128)(2,1)}, bf16[1024,512]{1,0:T(8,128)(2,1)S(1)}, u32[]{:S(2)}, u32[]{:S(2)}) collective-permute-start(bf16[1024,512]{1,0:T(8,128)(2,1)} %tokens.3), channel_id=1, source_target_pairs={{0,1},{1,0},{2,3},{3,2},{4,5},{5,4},{6,7},{7,6},{8,9},{9,8},{10,11... | collective-permute-start | bytes 3145736 | tf_op jit(solution)/shard_map/ppermute | solution.py:21
  0.5 1.4 %copy-start.5 = (bf16[1024,512]{1,0:T(8,128)(2,1)S(1)}, bf16[1024,512]{1,0:T(8,128)(2,1)}, u32[]{:S(2)}) copy-start(bf16[1024,512]{1,0:T(8,128)(2,1)} %tokens.3) | copy-start | bytes 3145732
  1.9 9.7 %collective-permute-start = (bf16[256,512]{1,0:T(8,128)(2,1)S(1)}, bf16[256,512]{1,0:T(8,128)(2,1)S(1)}, u32[]{:S(2)}, u32[]{:S(2)}) collective-permute-start(bf16[256,512]{1,0:T(8,128)(2,1)S(1)} %shard_map.73), channel_id=1, source_target_pairs={{0,2},{1,3},{2,0},{3,1},{4,6},{5,7},{6,4},{7,5},{8,10},{9,11},{10,... | collective-permute-start | bytes 786440 | tf_op jit(solution)/shard_map/ppermute | solution.py:21
  4.9 12.4 %collective-permute-start.3 = (bf16[256,512]{1,0:T(8,128)(2,1)S(1)}, bf16[256,512]{1,0:T(8,128)(2,1)S(1)}, u32[]{:S(2)}, u32[]{:S(2)}) collective-permute-start(bf16[256,512]{1,0:T(8,128)(2,1)S(1)} %get-tuple-element.50), channel_id=1, source_target_pairs={{0,2},{1,3},{2,0},{3,1},{4,6},{5,7},{6,4},{7,5},{8,10},{9,11},{10,... | collective-permute-start | bytes 786440 | tf_op jit(solution)/shard_map/ppermute | solution.py:21
  5.0 17.9 %collective-permute-start.5 = (bf16[256,512]{1,0:T(8,128)(2,1)S(1)}, bf16[256,512]{1,0:T(8,128)(2,1)S(1)}, u32[]{:S(2)}, u32[]{:S(2)}) collective-permute-start(bf16[256,512]{1,0:T(8,128)(2,1)S(1)} %get-tuple-element.55), channel_id=1, source_target_pairs={{0,2},{1,3},{2,0},{3,1},{4,6},{5,7},{6,4},{7,5},{8,10},{9,11},{10,... | collective-permute-start | bytes 786440 | tf_op jit(solution)/shard_map/ppermute | solution.py:21
  7.0 18.4 %collective-permute-start.7 = (bf16[128,512]{1,0:T(8,128)(2,1)S(1)}, bf16[128,512]{1,0:T(8,128)(2,1)S(1)}, u32[]{:S(2)}, u32[]{:S(2)}) collective-permute-start(bf16[128,512]{1,0:T(8,128)(2,1)S(1)} %get-tuple-element.60), channel_id=1, source_target_pairs={{0,2},{1,3},{2,0},{3,1},{4,6},{5,7},{6,4},{7,5},{8,10},{9,11},{10,... | collective-permute-start | bytes 393224 | tf_op jit(solution)/shard_map/ppermute | solution.py:21
  11.6 26.5 %collective-permute-start.1 = (bf16[256,512]{1,0:T(8,128)(2,1)S(1)}, bf16[256,512]{1,0:T(8,128)(2,1)S(1)}, u32[]{:S(2)}, u32[]{:S(2)}) collective-permute-start(bf16[256,512]{1,0:T(8,128)(2,1)S(1)} %collective-permute-done.refs_0_), channel_id=1, source_target_pairs={{0,1},{1,0},{2,3},{3,2},{4,5},{5,4},{6,7},{7,6},{8,9},{9,8},{10,11... | collective-permute-start | bytes 786440 | tf_op jit(solution)/shard_map/ppermute | solution.py:21
  17.2 22.7 %collective-permute-start.4 = (bf16[256,512]{1,0:T(8,128)(2,1)S(1)}, bf16[256,512]{1,0:T(8,128)(2,1)S(1)}, u32[]{:S(2)}, u32[]{:S(2)}) collective-permute-start(bf16[256,512]{1,0:T(8,128)(2,1)S(1)} %collective-permute-done.3.refs_0_), channel_id=1, source_target_pairs={{0,1},{1,0},{2,3},{3,2},{4,5},{5,4},{6,7},{7,6},{8,9},{9,8},{10,11... | collective-permute-start | bytes 786440 | tf_op jit(solution)/shard_map/ppermute | solution.py:21
  22.8 18.9 %collective-permute-start.6 = (bf16[256,512]{1,0:T(8,128)(2,1)S(1)}, bf16[256,512]{1,0:T(8,128)(2,1)S(1)}, u32[]{:S(2)}, u32[]{:S(2)}) collective-permute-start(bf16[256,512]{1,0:T(8,128)(2,1)S(1)} %collective-permute-done.5.refs_0_), channel_id=1, source_target_pairs={{0,1},{1,0},{2,3},{3,2},{4,5},{5,4},{6,7},{7,6},{8,9},{9,8},{10,11... | collective-permute-start | bytes 786440 | tf_op jit(solution)/shard_map/ppermute | solution.py:21
  25.3 5.2 %collective-permute-start.9 = (bf16[128,512]{1,0:T(8,128)(2,1)S(1)}, bf16[128,512]{1,0:T(8,128)(2,1)S(1)}, u32[]{:S(2)}, u32[]{:S(2)}) collective-permute-start(bf16[128,512]{1,0:T(8,128)(2,1)S(1)} %get-tuple-element.65), channel_id=1, source_target_pairs={{0,2},{1,3},{2,0},{3,1},{4,6},{5,7},{6,4},{7,5},{8,10},{9,11},{10,... | collective-permute-start | bytes 393224 | tf_op jit(solution)/shard_map/ppermute | solution.py:21
  30.5 13.0 %collective-permute-start.8 = (bf16[128,512]{1,0:T(8,128)(2,1)S(1)}, bf16[128,512]{1,0:T(8,128)(2,1)S(1)}, u32[]{:S(2)}, u32[]{:S(2)}) collective-permute-start(bf16[128,512]{1,0:T(8,128)(2,1)S(1)} %collective-permute-done.7.refs_0_), channel_id=1, source_target_pairs={{0,1},{1,0},{2,3},{3,2},{4,5},{5,4},{6,7},{7,6},{8,9},{9,8},{10,11... | collective-permute-start | bytes 393224 | tf_op jit(solution)/shard_map/ppermute | solution.py:21
  30.5 14.4 %collective-permute-start.10 = (bf16[128,512]{1,0:T(8,128)(2,1)S(1)}, bf16[128,512]{1,0:T(8,128)(2,1)S(1)}, u32[]{:S(2)}, u32[]{:S(2)}) collective-permute-start(bf16[128,512]{1,0:T(8,128)(2,1)S(1)} %collective-permute-done.9.refs_0_), channel_id=1, source_target_pairs={{0,1},{1,0},{2,3},{3,2},{4,5},{5,4},{6,7},{7,6},{8,9},{9,8},{10,11... | collective-permute-start | bytes 393224 | tf_op jit(solution)/shard_map/ppermute | solution.py:21
  31.0 1.6 %copy-start.1 = (bf16[2048,512]{1,0:T(8,128)(2,1)S(1)}, bf16[2048,512]{1,0:T(8,128)(2,1)}, u32[]{:S(2)}) copy-start(bf16[2048,512]{1,0:T(8,128)(2,1)} %refs_3_.11) | copy-start | bytes 6291460
  32.6 1.6 %copy-start.3 = (bf16[2048,512]{1,0:T(8,128)(2,1)S(1)}, bf16[2048,512]{1,0:T(8,128)(2,1)}, u32[]{:S(2)}) copy-start(bf16[2048,512]{1,0:T(8,128)(2,1)} %refs_2_.21) | copy-start | bytes 6291460
  34.2 3.9 %copy-start.2 = (bf16[2048,512]{1,0:T(8,128)(2,1)S(1)}, bf16[2048,512]{1,0:T(8,128)(2,1)}, u32[]{:S(2)}) copy-start(bf16[2048,512]{1,0:T(8,128)(2,1)} %refs_3_.11) | copy-start | bytes 6291460
  44.9 9.6 %copy-start.8 = (f32[4,16]{1,0:T(4,128)S(1)}, f32[4,16]{1,0:T(4,128)}, u32[]{:S(2)}) copy-start(f32[4,16]{1,0:T(4,128)} %table.1) | copy-start | bytes 772
  44.9 9.8 %copy-start.4 = (bf16[2048,512]{1,0:T(8,128)(2,1)S(1)}, bf16[2048,512]{1,0:T(8,128)(2,1)}, u32[]{:S(2)}) copy-start(bf16[2048,512]{1,0:T(8,128)(2,1)} %refs_2_.21) | copy-start | bytes 6291460
  44.9 9.8 %copy-start.6 = (s32[6,1024]{1,0:T(8,128)S(1)}, s32[6,1024]{1,0:T(8,128)}, u32[]{:S(2)}) copy-start(s32[6,1024]{1,0:T(8,128)} %refs_6_.9) | copy-start | bytes 73732
  45.7 5.5 %collective-permute-start.11 = (bf16[4,128,128]{2,1,0:T(8,128)(2,1)S(1)}, bf16[4,128,128]{2,1,0:T(8,128)(2,1)S(1)}, u32[]{:S(2)}, u32[]{:S(2)}) collective-permute-start(bf16[4,128,128]{2,1,0:T(8,128)(2,1)S(1)} %get-tuple-element.80), channel_id=1, source_target_pairs={{0,4},{4,0},{8,12},{12,8},{1,5},{5,1},{9,13},{13,9},{2,6},{6,2},{1... | collective-permute-start | bytes 393224 | tf_op jit(solution)/shard_map/ppermute | solution.py:21
  51.9 9.7 %collective-permute-start.12 = (bf16[4,128,128]{2,1,0:T(8,128)(2,1)S(1)}, bf16[4,128,128]{2,1,0:T(8,128)(2,1)S(1)}, u32[]{:S(2)}, u32[]{:S(2)}) collective-permute-start(bf16[4,128,128]{2,1,0:T(8,128)(2,1)S(1)} %get-tuple-element.82), channel_id=1, source_target_pairs={{0,8},{4,12},{8,0},{12,4},{1,9},{5,13},{9,1},{13,5},{2,10},{6,14},... | collective-permute-start | bytes 393224 | tf_op jit(solution)/shard_map/ppermute | solution.py:21
  60.4 1.2 %copy-start.7 = (f32[512]{0:T(512)S(1)}, f32[512]{0:T(512)}, u32[]{:S(2)}) copy-start(f32[512]{0:T(512)} %param.13) | copy-start | bytes 6148

commit v2 on v1

--- a/solution.py
+++ b/solution.py
@@ -8,12 +8,13 @@
 from jax.sharding import PartitionSpec as P
 
 
-CHUNKS = (2, 2, 2, 1, 1)
+CHUNKS = (3, 2, 2, 1)
 EPS = 1e-06
 F32 = jnp.float32
 BF16 = jnp.bfloat16
 VMEM = pl.BlockSpec(memory_space=pltpu.VMEM)
 ANY = pl.BlockSpec(memory_space=pl.ANY)
+HBM = pl.BlockSpec(memory_space=pltpu.HBM)
 
 
 def swap(block, axis, apart):
@@ -25,8 +26,8 @@
     return lax.dot_general(a, b, (dims, ((), ())), preferred_element_type=F32)
 
 
-def keep(array):
-    return pltpu.with_memory_space_constraint(array, pltpu.VMEM)
+def outside(array):
+    return pltpu.with_memory_space_constraint(array, pltpu.HBM)
 
 
 def call(kernel, outs, in_specs, args, out_specs=None, scratch=(), limit=8):
@@ -62,24 +63,44 @@
         copy.wait()
 
 
-def early_kernel(n_near, tile, *refs):
+def own_kernel(n_head, tokens, *refs):
     me = lax.axis_index("head")
-    pieces = refs[:n_near]
-    weights = refs[n_near : n_near + 3]
-    sums = refs[n_near + 3 :]
-    rows, depth = pieces[0].shape
-
-    def step(i, carry):
-        at = pl.ds(pl.multiple_of(i * tile, tile), tile)
-        for weight, total in zip(weights, sums):
-            acc = None
-            for offset, piece in enumerate(pieces):
-                part = dot(piece[at, :], weight_rows(me, weight, offset, depth))
-                acc = part if acc is None else acc + part
-            total[at, :] = acc
-        return carry
-
-    lax.fori_loop(0, rows // tile, step, 0)
+    sources, weights, sums = refs[:3], refs[3:6], refs[6:9]
+    held, held_sem, sems = refs[9:]
+    depth = tokens.shape[1]
+    fetch = pltpu.make_async_copy(tokens, held, held_sem)
+    fetch.start()
+
+    def copies(offset):
+        start = pl.multiple_of((me ^ offset) * depth, depth)
+        at = pl.ds(start, depth)
+        return [
+            pltpu.make_async_copy(source.at[at], weight.at[at], sems.at[offset, i])
+            for i, (source, weight) in enumerate(zip(sources, weights))
+        ]
+
+    loads = [copies(offset) for offset in range(n_head)]
+    for load in loads:
+        for copy in load:
+            copy.start()
+    fetch.wait()
+    for copy, weight, total in zip(loads[0], weights, sums):
+        copy.wait()
+        total[...] = dot(held[...], weight_rows(me, weight, 0, depth))
+    for load in loads[1:]:
+        for copy in load:
+            copy.wait()
+
+
+def near_kernel(n_near, *refs):
+    me = lax.axis_index("head")
+    pieces, weights, before, sums = refs[:n_near], refs[n_near : n_near + 3], refs[n_near + 3 : n_near + 6], refs[n_near + 6 :]
+    depth = pieces[0].shape[1]
+    for weight, total, grown in zip(weights, before, sums):
+        acc = total[...]
+        for i, piece in enumerate(pieces):
+            acc = acc + dot(piece[...], weight_rows(me, weight, 1 + i, depth))
+        grown[...] = acc
 
 
 def late_sum(base, pieces, weight, early, lo, rows):
@@ -98,9 +119,9 @@
     keys, values, state, state_low = refs[-4:]
     rows, width = keys.shape
     size = width // heads
+    raw_k = late_sum(base, pieces, k_weight, k_early, lo, rows)
     raw_v = late_sum(base, pieces, v_weight, v_early, lo, rows).astype(BF16)
     values[...] = raw_v
-    raw_k = late_sum(base, pieces, k_weight, k_early, lo, rows)
     for head in range(heads):
         cols = slice(head * size, (head + 1) * size)
         key = unit_rows(raw_k[:, cols])
@@ -171,10 +192,10 @@
             scaled[level][:, cols] = (wide * far[level][:, cols]).astype(BF16)
 
 
-def add_kernel(total, partner, grown, low):
+def add_kernel(total, partner, *grown):
     summed = total[...] + partner[...].astype(F32)
-    grown[...] = summed
-    low[...] = summed.astype(BF16)
+    for out in grown:
+        out[...] = summed.astype(out.dtype)
 
 
 def final_kernel(heads, depth, edges, *refs):
@@ -224,27 +245,33 @@
     for share in CHUNKS:
         edges.append(edges[-1] + share * unit)
     spans = list(zip(edges[:-1], edges[1:]))
-
-    q_weight, k_weight, v_weight = (keep(weight) for weight in (q_weight, k_weight, v_weight))
-
-    cuts = []
-    for group in (spans[:1], spans[1:]):
-        cuts += call(
-            functools.partial(cut_kernel, group),
-            [((hi - lo, feat_here), BF16) for lo, hi in group],
-            [ANY],
-            (tokens,),
-            scratch=[pltpu.SemaphoreType.DMA((len(group),))],
-        )
+    last = len(spans) - 1
+
+    cuts = [tokens[: spans[0][1]]]
+    cuts += call(
+        functools.partial(cut_kernel, spans[1:]),
+        [((hi - lo, feat_here), BF16) for lo, hi in spans[1:]],
+        [HBM],
+        (outside(tokens),),
+        scratch=[pltpu.SemaphoreType.DMA((last,))],
+    )
     far = [swap(piece, "head", base) for piece in cuts]
-    near = hop(tokens, base)
+    near = hop(tokens, base)[1:]
 
     big = (row_count, width)
+    *weights, q_own, k_own, v_own = call(
+        functools.partial(own_kernel, 2 * base),
+        [(q_weight.shape, BF16)] * 3 + [(big, F32)] * 3,
+        [HBM] * 4,
+        tuple(outside(array) for array in (tokens, q_weight, k_weight, v_weight)),
+        scratch=[pltpu.VMEM(tokens.shape, BF16), pltpu.SemaphoreType.DMA, pltpu.SemaphoreType.DMA((2 * base, 3))],
+    )
+    q_weight, k_weight, v_weight = weights
     early = call(
-        functools.partial(early_kernel, base, row_count // 4),
+        functools.partial(near_kernel, base - 1),
         [(big, F32)] * 3,
-        [VMEM] * (base + 3),
-        (*near, q_weight, k_weight, v_weight),
+        [VMEM] * (base + 5),
+        (*near, *weights, q_own, k_own, v_own),
     )
     table = call(table_kernel, [((2 * quant, width), BF16)], [VMEM], (level_table,))[0]
 
@@ -279,7 +306,9 @@
         merged.append(partner)
         if level + 1 < depth:
             shape = (heads, size, size)
-            total, low = call(add_kernel, [(shape, F32), (shape, BF16)], [VMEM, VMEM], (total, partner))
+            kinds = [(shape, BF16)] + [(shape, F32)] * (level + 2 < depth)
+            low, *rest = call(add_kernel, kinds, [VMEM, VMEM], (total, partner))
+            total = rest[0] if rest else None
 
     inputs = parts + [chunk[level] for level in range(depth) for chunk in scaled] + merged
     return call(

time: 63.3 us -> 59.3 us (0.937)
  local copies, waits for them, and re-layouts: 4.57 us -> 1.03 us
  Pallas kernels: 21.2 us -> 20.2 us
  waiting for transfers between devices: 25.5 us -> 26.2 us
    unnamed x18 -> x6, local copies, waits for them, and re-layouts: 4.57 us -> 0.01 us
    slice x0 -> x1, local copies, waits for them, and re-layouts: none -> 1.02 us  [on_device(): cuts = [tokens[:spans[0][1]]]]
    pallas_call x16 -> x14, Pallas kernels: 21.2 us -> 20.2 us  [call(): pl.pallas_call(kernel, out_shape=kept if out_specs is None else [jax.Shap...]
    ppermute x13 -> x11, waiting for transfers between devices: 25.5 us -> 26.2 us  [swap(): return lax.ppermute(block, axis, route)]
    ppermute x13 -> x11, starting transfers between devices: 11.8 us -> 11.6 us  [swap(): return lax.ppermute(block, axis, route)]
  transfers between devices with their start and end apart: 13 -> 11, of which waited for: 6 -> 5; matrix products, arithmetic and copies ran while one was open for 0% -> 2% of each run, Pallas kernels for 29% -> 30%
where the time goes in v2:
time: 59.3 us; the launch traced here: 59.1 us
  waiting for transfers between devices  26.2 us (44%)
  Pallas kernels  20.2 us (34%)
  starting transfers between devices  11.6 us (20%)
  local copies, waits for them, and re-layouts  1.03 us (2%)
    ppermute x11, waiting for transfers between devices, swap(): return lax.ppermute(block, axis, route)  26.2 us
    pallas_call x14, Pallas kernels, call(): pl.pallas_call(kernel, out_shape=kept if out_specs is None else [jax.Shap...  20.2 us
    ppermute x11, starting transfers between devices, swap(): return lax.ppermute(block, axis, route)  11.6 us
  transfers between devices with their start and end apart: 11, of which 5 were waited for; matrix products, arithmetic and copies ran while one was open for 2% of the time, Pallas kernels for 30%

profile of v2, /device:TPU:0, one launch (start us, length us, event | category | flops | bytes accessed | tf_op | source)
XLA Modules:
  0.0 59.1 jit_solution(17070278687789776395)
XLA Ops:
  0.0 0.5 collective-permute-start.2
  0.5 1.0 %slice.3 = bf16[384,512]{1,0:T(8,128)(2,1)S(1)} slice(bf16[1024,512]{1,0:T(8,128)(2,1)} %tokens.3), slice={[0:384], [0:512]} | slice | bytes 786432 | tf_op jit(solution)/shard_map/slice | solution.py:250
  1.5 2.5 %collective-permute-start = (bf16[384,512]{1,0:T(8,128)(2,1)S(1)}, bf16[384,512]{1,0:T(8,128)(2,1)S(1)}, u32[]{:S(2)}, u32[]{:S(2)}) collective-permute-start(bf16[384,512]{1,0:T(8,128)(2,1)S(1)} %slice.3), channel_id=1, source_target_pairs={{0,2},{1,3},{2,0},{3,1},{4,6},{5,7},{6,4},{7,5},{8,10},{9,11},{10,... | collective-permute-start | bytes 1179656 | tf_op jit(solution)/shard_map/ppermute | solution.py:22
  4.1 1.1 %shard_map.78 = (bf16[256,512]{1,0:T(8,128)(2,1)S(1)}, bf16[256,512]{1,0:T(8,128)(2,1)S(1)}, bf16[128,512]{1,0:T(8,128)(2,1)S(1)}) custom-call(bf16[1024,512]{1,0:T(8,128)(2,1)} %tokens.3), custom_call_target="tpu_custom_call" | custom-call | tf_op jit(solution)/shard_map/pallas_call | solution.py:35
  5.2 0.1 collective-permute-start.3
  5.2 2.0 %collective-permute-start.5 = (bf16[256,512]{1,0:T(8,128)(2,1)S(1)}, bf16[256,512]{1,0:T(8,128)(2,1)S(1)}, u32[]{:S(2)}, u32[]{:S(2)}) collective-permute-start(bf16[256,512]{1,0:T(8,128)(2,1)S(1)} %get-tuple-element.59), channel_id=1, source_target_pairs={{0,2},{1,3},{2,0},{3,1},{4,6},{5,7},{6,4},{7,5},{8,10},{9,11},{10,... | collective-permute-start | bytes 786440 | tf_op jit(solution)/shard_map/ppermute | solution.py:22
  7.2 6.8 %collective-permute-done.refs_0_ = bf16[384,512]{1,0:T(8,128)(2,1)S(1)} collective-permute-done((bf16[384,512]{1,0:T(8,128)(2,1)S(1)}, bf16[384,512]{1,0:T(8,128)(2,1)S(1)}, u32[]{:S(2)}, u32[]{:S(2)}) %collective-permute-start) | collective-permute-done | bytes 393248 | tf_op jit(solution)/shard_map/ppermute | solution.py:22
  14.0 0.0 collective-permute-start.1
  14.0 5.6 %collective-permute-done.3.refs_0_ = bf16[256,512]{1,0:T(8,128)(2,1)S(1)} collective-permute-done((bf16[256,512]{1,0:T(8,128)(2,1)S(1)}, bf16[256,512]{1,0:T(8,128)(2,1)S(1)}, u32[]{:S(2)}, u32[]{:S(2)}) %collective-permute-start.3) | collective-permute-done | bytes 262176 | tf_op jit(solution)/shard_map/ppermute | solution.py:22
  19.6 0.0 collective-permute-start.4
  19.6 5.4 %collective-permute-done.5.refs_0_ = bf16[256,512]{1,0:T(8,128)(2,1)S(1)} collective-permute-done((bf16[256,512]{1,0:T(8,128)(2,1)S(1)}, bf16[256,512]{1,0:T(8,128)(2,1)S(1)}, u32[]{:S(2)}, u32[]{:S(2)}) %collective-permute-start.5) | collective-permute-done | bytes 262176 | tf_op jit(solution)/shard_map/ppermute | solution.py:22
  25.1 0.0 collective-permute-start.6
  25.1 1.7 %collective-permute-start.7 = (bf16[128,512]{1,0:T(8,128)(2,1)S(1)}, bf16[128,512]{1,0:T(8,128)(2,1)S(1)}, u32[]{:S(2)}, u32[]{:S(2)}) collective-permute-start(bf16[128,512]{1,0:T(8,128)(2,1)S(1)} %get-tuple-element.64), channel_id=1, source_target_pairs={{0,2},{1,3},{2,0},{3,1},{4,6},{5,7},{6,4},{7,5},{8,10},{9,11},{10,... | collective-permute-start | bytes 393224 | tf_op jit(solution)/shard_map/ppermute | solution.py:22
  26.8 4.2 %collective-permute-done.7.refs_0_ = bf16[128,512]{1,0:T(8,128)(2,1)S(1)} collective-permute-done((bf16[128,512]{1,0:T(8,128)(2,1)S(1)}, bf16[128,512]{1,0:T(8,128)(2,1)S(1)}, u32[]{:S(2)}, u32[]{:S(2)}) %collective-permute-start.7) | collective-permute-done | bytes 131104 | tf_op jit(solution)/shard_map/ppermute | solution.py:22
  31.0 0.0 collective-permute-start.8
  31.0 3.6 %shard_map.73 = (bf16[2048,512]{1,0:T(8,128)(2,1)S(1)}, bf16[2048,512]{1,0:T(8,128)(2,1)S(1)}, bf16[2048,512]{1,0:T(8,128)(2,1)S(1)}, f32[1024,512]{1,0:T(8,128)...) custom-call(bf16[1024,512]{1,0:T(8,128)(2,1)} %tokens.3, bf16[2048,512]{1,0:T(8,128)(2,1)} %refs_0_.1, ...), custom_call_target="tpu_custom_call" | custom-call | tf_op jit(solution)/shard_map/pallas_call | solution.py:35
  34.6 0.0 collective-permute-done.2.refs_0_
  34.6 1.8 %shard_map.74 = (f32[1024,512]{1,0:T(8,128)S(1)}, f32[1024,512]{1,0:T(8,128)S(1)}, f32[1024,512]{1,0:T(8,128)S(1)}) custom-call(bf16[1024,512]{1,0:T(8,128)(2,1)S(1)} %collective-permute-done.2.refs_0_, bf16[2048,512]{1,0:T(8,128)(2,1)S(1)} %get-tuple-element.42.refs_1_.refs_2_, bf16[2048,512]{1,0:T(8,128)(2,1)S(1)} %get-tuple-element.43.refs_2_, ...), custom_call_target="tpu_custom_call" | custom-call | tf_op jit(solution)/shard_map/pallas_call | solution.py:35
  36.4 0.0 collective-permute-done.1.refs_1_
  36.4 1.9 %shard_map.75 = (bf16[384,512]{1,0:T(8,128)(2,1)S(1)}, bf16[384,512]{1,0:T(8,128)(2,1)S(1)}, f32[4,128,128]{2,1,0:T(8,128)S(1)}, bf16[4,128,128]{2,1,0:T(8,128)(2,1)}) custom-call(bf16[384,512]{1,0:T(8,128)(2,1)S(1)} %collective-permute-done.refs_0_, bf16[384,512]{1,0:T(8,128)(2,1)S(1)} %collective-permute-done.1.refs_1_, ...), custom_call_target="tpu_custom_call" | custom-call | tf_op jit(solution)/shard_map/pallas_call | solution.py:35
  38.3 0.0 collective-permute-done.4.refs_1_
  38.3 1.6 %shard_map.79 = (bf16[256,512]{1,0:T(8,128)(2,1)S(1)}, bf16[256,512]{1,0:T(8,128)(2,1)S(1)}, f32[4,128,128]{2,1,0:T(8,128)S(1)}, bf16[4,128,128]{2,1,0:T(8,128)(2,1)}) custom-call(bf16[256,512]{1,0:T(8,128)(2,1)S(1)} %collective-permute-done.3.refs_0_, bf16[256,512]{1,0:T(8,128)(2,1)S(1)} %collective-permute-done.4.refs_1_, ...), custom_call_target="tpu_custom_call" | custom-call | tf_op jit(solution)/shard_map/pallas_call | solution.py:35
  39.9 0.0 collective-permute-done.6.refs_1_
  39.9 1.6 %shard_map.81 = (bf16[256,512]{1,0:T(8,128)(2,1)S(1)}, bf16[256,512]{1,0:T(8,128)(2,1)S(1)}, f32[4,128,128]{2,1,0:T(8,128)S(1)}, bf16[4,128,128]{2,1,0:T(8,128)(2,1)}) custom-call(bf16[256,512]{1,0:T(8,128)(2,1)S(1)} %collective-permute-done.5.refs_0_, bf16[256,512]{1,0:T(8,128)(2,1)S(1)} %collective-permute-done.6.refs_1_, ...), custom_call_target="tpu_custom_call" | custom-call | tf_op jit(solution)/shard_map/pallas_call | solution.py:35
  41.5 0.0 collective-permute-done.8.refs_1_
  41.5 0.0 copy-start.2
  41.5 0.0 copy-start
  41.5 0.6 %shard_map.83 = (bf16[128,512]{1,0:T(8,128)(2,1)S(1)}, bf16[128,512]{1,0:T(8,128)(2,1)S(1)}, f32[4,128,128]{2,1,0:T(8,128)S(1)}, bf16[4,128,128]{2,1,0:T(8,128)(2,1)S(1)}) custom-call(bf16[128,512]{1,0:T(8,128)(2,1)S(1)} %collective-permute-done.7.refs_0_, bf16[128,512]{1,0:T(8,128)(2,1)S(1)} %collective-permute-done.8.refs_1_, ...), custom_call_target="tpu_custom_call" | custom-call | tf_op jit(solution)/shard_map/pallas_call | solution.py:35
  42.1 1.9 %collective-permute-start.9 = (bf16[4,128,128]{2,1,0:T(8,128)(2,1)S(1)}, bf16[4,128,128]{2,1,0:T(8,128)(2,1)S(1)}, u32[]{:S(2)}, u32[]{:S(2)}) collective-permute-start(bf16[4,128,128]{2,1,0:T(8,128)(2,1)S(1)} %get-tuple-element.77), channel_id=1, source_target_pairs={{0,4},{4,0},{8,12},{12,8},{1,5},{5,1},{9,13},{13,9},{2,6},{6,2},{1... | collective-permute-start | bytes 393224 | tf_op jit(solution)/shard_map/ppermute | solution.py:22
  44.0 4.2 %collective-permute-done.9.partner.refs_12_ = bf16[4,128,128]{2,1,0:T(8,128)(2,1)S(1)} collective-permute-done((bf16[4,128,128]{2,1,0:T(8,128)(2,1)S(1)}, bf16[4,128,128]{2,1,0:T(8,128)(2,1)S(1)}, u32[]{:S(2)}, u32[]{:S(2)}) %collective-permute-start.9) | collective-permute-done | bytes 131104 | tf_op jit(solution)/shard_map/ppermute | solution.py:22
  48.2 2.8 %collective-permute-start.10 = (bf16[4,128,128]{2,1,0:T(8,128)(2,1)S(1)}, bf16[4,128,128]{2,1,0:T(8,128)(2,1)S(1)}, u32[]{:S(2)}, u32[]{:S(2)}) collective-permute-start(bf16[4,128,128]{2,1,0:T(8,128)(2,1)S(1)} %shard_map.85), channel_id=1, source_target_pairs={{0,8},{4,12},{8,0},{12,4},{1,9},{5,13},{9,1},{13,5},{2,10},{6,14},... | collective-permute-start | bytes 393224 | tf_op jit(solution)/shard_map/ppermute | solution.py:22
  51.0 0.0 copy-done.2
  51.0 0.2 shard_map.76.refs_7_
  51.2 0.0 copy-done
  51.2 1.1 %shard_map.84 = (f32[128,512]{1,0:T(8,128)S(1)}, bf16[128,512]{1,0:T(8,128)(2,1)S(1)}, bf16[128,512]{1,0:T(8,128)(2,1)S(1)}) custom-call(bf16[128,512]{1,0:T(8,128)(2,1)S(1)} %collective-permute-done.7.refs_0_, bf16[128,512]{1,0:T(8,128)(2,1)S(1)} %collective-permute-done.8.refs_1_, bf16[2048,512]{1,0:T(8,128)(2,1)S(1)} %get-tuple-element.42.refs_1_.refs_2_, ...), custom_call_target="tpu_custom_call" | custom-call | tf_op jit(solution)/shard_map/pallas_call | solution.py:35
  52.4 1.4 %shard_map.82 = (f32[256,512]{1,0:T(8,128)S(1)}, bf16[256,512]{1,0:T(8,128)(2,1)S(1)}, bf16[256,512]{1,0:T(8,128)(2,1)S(1)}) custom-call(bf16[256,512]{1,0:T(8,128)(2,1)S(1)} %collective-permute-done.5.refs_0_, bf16[256,512]{1,0:T(8,128)(2,1)S(1)} %collective-permute-done.6.refs_1_, bf16[2048,512]{1,0:T(8,128)(2,1)S(1)} %get-tuple-element.42.refs_1_.refs_2_, ...), custom_call_target="tpu_custom_call" | custom-call | tf_op jit(solution)/shard_map/pallas_call | solution.py:35
  53.8 1.4 %shard_map.80 = (f32[256,512]{1,0:T(8,128)S(1)}, bf16[256,512]{1,0:T(8,128)(2,1)S(1)}, bf16[256,512]{1,0:T(8,128)(2,1)S(1)}) custom-call(bf16[256,512]{1,0:T(8,128)(2,1)S(1)} %collective-permute-done.3.refs_0_, bf16[256,512]{1,0:T(8,128)(2,1)S(1)} %collective-permute-done.4.refs_1_, bf16[2048,512]{1,0:T(8,128)(2,1)S(1)} %get-tuple-element.42.refs_1_.refs_2_, ...), custom_call_target="tpu_custom_call" | custom-call | tf_op jit(solution)/shard_map/pallas_call | solution.py:35
  55.2 0.0 copy-start.1
  55.3 2.2 %shard_map.77 = (f32[384,512]{1,0:T(8,128)S(1)}, bf16[384,512]{1,0:T(8,128)(2,1)S(1)}, bf16[384,512]{1,0:T(8,128)(2,1)S(1)}) custom-call(bf16[384,512]{1,0:T(8,128)(2,1)S(1)} %collective-permute-done.refs_0_, bf16[384,512]{1,0:T(8,128)(2,1)S(1)} %collective-permute-done.1.refs_1_, bf16[2048,512]{1,0:T(8,128)(2,1)S(1)} %get-tuple-element.42.refs_1_.refs_2_, ...), custom_call_target="tpu_custom_call" | custom-call | tf_op jit(solution)/shard_map/pallas_call | solution.py:35
  57.5 0.0 collective-permute-done.10.refs_13_
  57.5 0.0 copy-done.1
  57.5 1.6 %shard_map.86 = bf16[1024,512]{1,0:T(8,128)(2,1)} custom-call(f32[384,512]{1,0:T(8,128)S(1)} %get-tuple-element.53.refs_0_, f32[256,512]{1,0:T(8,128)S(1)} %get-tuple-element.58.refs_1_, f32[256,512]{1,0:T(8,128)S(1)} %get-tuple-element.63.refs_2_, f32[128,512]{1,0:T(8,128)S(1)} %get-tuple-element.68.refs_3_, ...), custom_call_target="tpu_custom_call" | custom-call | tf_op jit(solution)/shard_map/pallas_call | solution.py:35
  (1 shorter events, 0.0 us)
Async XLA Ops:
  0.0 34.6 %collective-permute-start.2 = (bf16[1024,512]{1,0:T(8,128)(2,1)}, bf16[1024,512]{1,0:T(8,128)(2,1)S(1)}, u32[]{:S(2)}, u32[]{:S(2)}) collective-permute-start(bf16[1024,512]{1,0:T(8,128)(2,1)} %tokens.3), channel_id=1, source_target_pairs={{0,1},{1,0},{2,3},{3,2},{4,5},{5,4},{6,7},{7,6},{8,9},{9,8},{10,11... | collective-permute-start | bytes 3145736 | tf_op jit(solution)/shard_map/ppermute | solution.py:22
  1.5 12.5 %collective-permute-start = (bf16[384,512]{1,0:T(8,128)(2,1)S(1)}, bf16[384,512]{1,0:T(8,128)(2,1)S(1)}, u32[]{:S(2)}, u32[]{:S(2)}) collective-permute-start(bf16[384,512]{1,0:T(8,128)(2,1)S(1)} %slice.3), channel_id=1, source_target_pairs={{0,2},{1,3},{2,0},{3,1},{4,6},{5,7},{6,4},{7,5},{8,10},{9,11},{10,... | collective-permute-start | bytes 1179656 | tf_op jit(solution)/shard_map/ppermute | solution.py:22
  5.2 14.5 %collective-permute-start.3 = (bf16[256,512]{1,0:T(8,128)(2,1)S(1)}, bf16[256,512]{1,0:T(8,128)(2,1)S(1)}, u32[]{:S(2)}, u32[]{:S(2)}) collective-permute-start(bf16[256,512]{1,0:T(8,128)(2,1)S(1)} %get-tuple-element.54), channel_id=1, source_target_pairs={{0,2},{1,3},{2,0},{3,1},{4,6},{5,7},{6,4},{7,5},{8,10},{9,11},{10,... | collective-permute-start | bytes 786440 | tf_op jit(solution)/shard_map/ppermute | solution.py:22
  5.2 19.8 %collective-permute-start.5 = (bf16[256,512]{1,0:T(8,128)(2,1)S(1)}, bf16[256,512]{1,0:T(8,128)(2,1)S(1)}, u32[]{:S(2)}, u32[]{:S(2)}) collective-permute-start(bf16[256,512]{1,0:T(8,128)(2,1)S(1)} %get-tuple-element.59), channel_id=1, source_target_pairs={{0,2},{1,3},{2,0},{3,1},{4,6},{5,7},{6,4},{7,5},{8,10},{9,11},{10,... | collective-permute-start | bytes 786440 | tf_op jit(solution)/shard_map/ppermute | solution.py:22
  14.0 22.4 %collective-permute-start.1 = (bf16[384,512]{1,0:T(8,128)(2,1)S(1)}, bf16[384,512]{1,0:T(8,128)(2,1)S(1)}, u32[]{:S(2)}, u32[]{:S(2)}) collective-permute-start(bf16[384,512]{1,0:T(8,128)(2,1)S(1)} %collective-permute-done.refs_0_), channel_id=1, source_target_pairs={{0,1},{1,0},{2,3},{3,2},{4,5},{5,4},{6,7},{7,6},{8,9},{9,8},{10,11... | collective-permute-start | bytes 1179656 | tf_op jit(solution)/shard_map/ppermute | solution.py:22
  19.6 18.7 %collective-permute-start.4 = (bf16[256,512]{1,0:T(8,128)(2,1)S(1)}, bf16[256,512]{1,0:T(8,128)(2,1)S(1)}, u32[]{:S(2)}, u32[]{:S(2)}) collective-permute-start(bf16[256,512]{1,0:T(8,128)(2,1)S(1)} %collective-permute-done.3.refs_0_), channel_id=1, source_target_pairs={{0,1},{1,0},{2,3},{3,2},{4,5},{5,4},{6,7},{7,6},{8,9},{9,8},{10,11... | collective-permute-start | bytes 786440 | tf_op jit(solution)/shard_map/ppermute | solution.py:22
  25.1 14.8 %collective-permute-start.6 = (bf16[256,512]{1,0:T(8,128)(2,1)S(1)}, bf16[256,512]{1,0:T(8,128)(2,1)S(1)}, u32[]{:S(2)}, u32[]{:S(2)}) collective-permute-start(bf16[256,512]{1,0:T(8,128)(2,1)S(1)} %collective-permute-done.5.refs_0_), channel_id=1, source_target_pairs={{0,1},{1,0},{2,3},{3,2},{4,5},{5,4},{6,7},{7,6},{8,9},{9,8},{10,11... | collective-permute-start | bytes 786440 | tf_op jit(solution)/shard_map/ppermute | solution.py:22
  25.1 5.9 %collective-permute-start.7 = (bf16[128,512]{1,0:T(8,128)(2,1)S(1)}, bf16[128,512]{1,0:T(8,128)(2,1)S(1)}, u32[]{:S(2)}, u32[]{:S(2)}) collective-permute-start(bf16[128,512]{1,0:T(8,128)(2,1)S(1)} %get-tuple-element.64), channel_id=1, source_target_pairs={{0,2},{1,3},{2,0},{3,1},{4,6},{5,7},{6,4},{7,5},{8,10},{9,11},{10,... | collective-permute-start | bytes 393224 | tf_op jit(solution)/shard_map/ppermute | solution.py:22
  31.0 10.5 %collective-permute-start.8 = (bf16[128,512]{1,0:T(8,128)(2,1)S(1)}, bf16[128,512]{1,0:T(8,128)(2,1)S(1)}, u32[]{:S(2)}, u32[]{:S(2)}) collective-permute-start(bf16[128,512]{1,0:T(8,128)(2,1)S(1)} %collective-permute-done.7.refs_0_), channel_id=1, source_target_pairs={{0,1},{1,0},{2,3},{3,2},{4,5},{5,4},{6,7},{7,6},{8,9},{9,8},{10,11... | collective-permute-start | bytes 393224 | tf_op jit(solution)/shard_map/ppermute | solution.py:22
  41.5 9.5 %copy-start.2 = (f32[4,16]{1,0:T(4,128)S(1)}, f32[4,16]{1,0:T(4,128)}, u32[]{:S(2)}) copy-start(f32[4,16]{1,0:T(4,128)} %table.1) | copy-start | bytes 772
  41.5 9.7 %copy-start = (s32[6,1024]{1,0:T(8,128)S(1)}, s32[6,1024]{1,0:T(8,128)}, u32[]{:S(2)}) copy-start(s32[6,1024]{1,0:T(8,128)} %refs_6_.7) | copy-start | bytes 73732
  42.1 6.1 %collective-permute-start.9 = (bf16[4,128,128]{2,1,0:T(8,128)(2,1)S(1)}, bf16[4,128,128]{2,1,0:T(8,128)(2,1)S(1)}, u32[]{:S(2)}, u32[]{:S(2)}) collective-permute-start(bf16[4,128,128]{2,1,0:T(8,128)(2,1)S(1)} %get-tuple-element.77), channel_id=1, source_target_pairs={{0,4},{4,0},{8,12},{12,8},{1,5},{5,1},{9,13},{13,9},{2,6},{6,2},{1... | collective-permute-start | bytes 393224 | tf_op jit(solution)/shard_map/ppermute | solution.py:22
  48.2 9.2 %collective-permute-start.10 = (bf16[4,128,128]{2,1,0:T(8,128)(2,1)S(1)}, bf16[4,128,128]{2,1,0:T(8,128)(2,1)S(1)}, u32[]{:S(2)}, u32[]{:S(2)}) collective-permute-start(bf16[4,128,128]{2,1,0:T(8,128)(2,1)S(1)} %shard_map.85), channel_id=1, source_target_pairs={{0,8},{4,12},{8,0},{12,4},{1,9},{5,13},{9,1},{13,5},{2,10},{6,14},... | collective-permute-start | bytes 393224 | tf_op jit(solution)/shard_map/ppermute | solution.py:22
  55.2 2.2 %copy-start.1 = (f32[512]{0:T(512)S(1)}, f32[512]{0:T(512)}, u32[]{:S(2)}) copy-start(f32[512]{0:T(512)} %param.13) | copy-start | bytes 6148

commit v3 on v2

--- a/solution.py
+++ b/solution.py
@@ -8,7 +8,7 @@
 from jax.sharding import PartitionSpec as P
 
 
-CHUNKS = (3, 2, 2, 1)
+CHUNKS = (1, 5, 5, 3, 2)
 EPS = 1e-06
 F32 = jnp.float32
 BF16 = jnp.bfloat16
@@ -51,12 +51,12 @@
     return (raw * lax.rsqrt(jnp.sum(raw * raw, -1, keepdims=True) + EPS)).astype(BF16)
 
 
-def cut_kernel(spans, tokens, *refs):
-    count = len(spans)
+def cut_kernel(boxes, tokens, *refs):
+    count = len(boxes)
     outs, sems = refs[:count], refs[count]
     copies = []
-    for i, (lo, hi) in enumerate(spans):
-        copy = pltpu.make_async_copy(tokens.at[lo:hi], outs[i], sems.at[i])
+    for i, (lo, hi, wide) in enumerate(boxes):
+        copy = pltpu.make_async_copy(tokens.at[lo:hi, :wide], outs[i], sems.at[i])
         copy.start()
         copies.append(copy)
     for copy in copies:
@@ -198,24 +198,37 @@
         out[...] = summed.astype(out.dtype)
 
 
-def final_kernel(heads, depth, edges, *refs):
+def fold_kernel(heads, levels, edges, *refs):
     count = len(edges) - 1
     parts = refs[:count]
-    scaled = [refs[count * (1 + level) : count * (2 + level)] for level in range(depth)]
-    refs = refs[count * (1 + depth) :]
-    merged = refs[:depth]
-    gain, out, done, sems = refs[depth:]
+    scaled = [refs[count * (1 + level) : count * (2 + level)] for level in range(levels)]
+    merged = refs[count * (1 + levels) :][:levels]
+    total = refs[-1]
+    size = total.shape[1] // heads
+    for i in range(count):
+        rows = slice(edges[i], edges[i + 1])
+        for head in range(heads):
+            cols = slice(head * size, (head + 1) * size)
+            acc = parts[i][:, cols]
+            for level in range(levels):
+                acc = acc + dot(scaled[level][i][:, cols], merged[level][head])
+            total[rows, cols] = acc
+
+
+def final_kernel(heads, edges, *refs):
+    count = len(edges) - 1
+    scaled = refs[:count]
+    before, merged, gain, out, done, sems = refs[count:]
     size = done.shape[1] // heads
+    share = jnp.full((size, size), 1.0 / size, BF16)
     copies = []
     for i in range(count):
         rows = slice(edges[i], edges[i + 1])
         for head in range(heads):
             cols = slice(head * size, (head + 1) * size)
-            total = parts[i][:, cols]
-            for level in range(depth):
-                total = total + dot(scaled[level][i][:, cols], merged[level][head])
-            total = total * lax.rsqrt(jnp.mean(total * total, -1, keepdims=True) + EPS)
-            done[rows, cols] = (total * gain[0:1, cols]).astype(BF16)
+            total = before[rows, cols] + dot(scaled[i][:, cols], merged[head])
+            mean = dot((total * total).astype(BF16), share)
+            done[rows, cols] = (total * lax.rsqrt(mean + EPS) * gain[0:1, cols]).astype(BF16)
         copy = pltpu.make_async_copy(done.at[rows], out.at[rows], sems.at[i])
         copy.start()
         copies.append(copy)
@@ -245,16 +258,18 @@
     for share in CHUNKS:
         edges.append(edges[-1] + share * unit)
     spans = list(zip(edges[:-1], edges[1:]))
-    last = len(spans) - 1
 
     cuts = [tokens[: spans[0][1]]]
-    cuts += call(
-        functools.partial(cut_kernel, spans[1:]),
-        [((hi - lo, feat_here), BF16) for lo, hi in spans[1:]],
+    boxes = [(lo, hi, feat_here) for lo, hi in spans[1:]] + [(0, 16, 128)]
+    *rest, small = call(
+        functools.partial(cut_kernel, boxes),
+        [((hi - lo, wide), BF16) for lo, hi, wide in boxes],
         [HBM],
         (outside(tokens),),
-        scratch=[pltpu.SemaphoreType.DMA((last,))],
+        scratch=[pltpu.SemaphoreType.DMA((len(boxes),))],
     )
+    cuts += rest
+    greetings = [swap(small, "seq", 1 << level) for level in range(depth)]
     far = [swap(piece, "head", base) for piece in cuts]
     near = hop(tokens, base)[1:]
 
@@ -310,12 +325,16 @@
             low, *rest = call(add_kernel, kinds, [VMEM, VMEM], (total, partner))
             total = rest[0] if rest else None
 
-    inputs = parts + [chunk[level] for level in range(depth) for chunk in scaled] + merged
+    inputs = parts + [chunk[level] for level in range(depth - 1) for chunk in scaled] + merged[:-1] + greetings
+    before = call(
+        functools.partial(fold_kernel, heads, depth - 1, edges), [(big, F32)], [VMEM] * len(inputs), inputs
+    )[0]
+    inputs = [chunk[-1] for chunk in scaled] + [before, merged[-1], out_gain.reshape(1, width)]
     return call(
-        functools.partial(final_kernel, heads, depth, edges),
+        functools.partial(final_kernel, heads, edges),
         [(big, BF16)],
-        [VMEM] * (len(inputs) + 1),
-        (*inputs, out_gain.reshape(1, width)),
+        [VMEM] * len(inputs),
+        inputs,
         out_specs=[ANY],
         scratch=[pltpu.VMEM(big, BF16), pltpu.SemaphoreType.DMA((len(spans),))],
     )[0]

time: 59.3 us -> 63.9 us (1.078)
  starting transfers between devices: 11.6 us -> 15.5 us
  Pallas kernels: 20.2 us -> 23.3 us
  waiting for transfers between devices: 26.2 us -> 23.8 us
    ppermute x11 -> x15, starting transfers between devices: 11.6 us -> 15.5 us  [swap(): return lax.ppermute(block, axis, route)]
    pallas_call x14 -> x17, Pallas kernels: 20.2 us -> 23.3 us  [call(): pl.pallas_call(kernel, out_shape=kept if out_specs is None else [jax.Shap...]
    ppermute x11 -> x15, waiting for transfers between devices: 26.2 us -> 23.8 us  [swap(): return lax.ppermute(block, axis, route)]
  transfers between devices with their start and end apart: 11 -> 15, of which waited for: 5 -> 5; matrix products, arithmetic and copies ran while one was open for 2% -> 1% of each run, Pallas kernels for 30% -> 33%
where the time goes in v3:
time: 63.9 us; the launch traced here: 63.7 us
  waiting for transfers between devices  23.8 us (37%)
  Pallas kernels  23.3 us (36%)
  starting transfers between devices  15.5 us (24%)
  local copies, waits for them, and re-layouts  1.07 us (2%)
    ppermute x15, waiting for transfers between devices, swap(): return lax.ppermute(block, axis, route)  23.8 us
    pallas_call x17, Pallas kernels, call(): pl.pallas_call(kernel, out_shape=kept if out_specs is None else [jax.Shap...  23.3 us
    ppermute x15, starting transfers between devices, swap(): return lax.ppermute(block, axis, route)  15.5 us
  transfers between devices with their start and end apart: 15, of which 5 were waited for; matrix products, arithmetic and copies ran while one was open for 1% of the time, Pallas kernels for 33%

profile of v3, /device:TPU:0, one launch (start us, length us, event | category | flops | bytes accessed | tf_op | source)
XLA Modules:
  0.0 63.7 jit_solution(16019652716630779592)
XLA Ops:
  0.0 0.5 collective-permute-start.2
  0.5 1.2 %shard_map.78 = (bf16[320,512]{1,0:T(8,128)(2,1)S(1)}, bf16[320,512]{1,0:T(8,128)(2,1)S(1)}, bf16[192,512]{1,0:T(8,128)(2,1)S(1)}, bf16[128,512]{1,0:T(8,128)(2,1)S(1)}, bf16[16,128]{1,0:T(8,128)(2,1)S(1)}) custom-call(bf16[1024,512]{1,0:T(8,128)(2,1)} %tokens.3), custom_call_target="tpu_custom_call" | custom-call | tf_op jit(solution)/shard_map/pallas_call | solution.py:35
  1.7 2.5 %collective-permute-start.3 = (bf16[320,512]{1,0:T(8,128)(2,1)S(1)}, bf16[320,512]{1,0:T(8,128)(2,1)S(1)}, u32[]{:S(2)}, u32[]{:S(2)}) collective-permute-start(bf16[320,512]{1,0:T(8,128)(2,1)S(1)} %get-tuple-element.62), channel_id=1, source_target_pairs={{0,2},{1,3},{2,0},{3,1},{4,6},{5,7},{6,4},{7,5},{8,10},{9,11},{10,... | collective-permute-start | bytes 983048 | tf_op jit(solution)/shard_map/ppermute | solution.py:22
  4.2 0.1 collective-permute-start.5
  4.3 1.9 %collective-permute-start.7 = (bf16[192,512]{1,0:T(8,128)(2,1)S(1)}, bf16[192,512]{1,0:T(8,128)(2,1)S(1)}, u32[]{:S(2)}, u32[]{:S(2)}) collective-permute-start(bf16[192,512]{1,0:T(8,128)(2,1)S(1)} %get-tuple-element.72), channel_id=1, source_target_pairs={{0,2},{1,3},{2,0},{3,1},{4,6},{5,7},{6,4},{7,5},{8,10},{9,11},{10,... | collective-permute-start | bytes 589832 | tf_op jit(solution)/shard_map/ppermute | solution.py:22
  6.3 6.5 %collective-permute-done.3.refs_0_ = bf16[320,512]{1,0:T(8,128)(2,1)S(1)} collective-permute-done((bf16[320,512]{1,0:T(8,128)(2,1)S(1)}, bf16[320,512]{1,0:T(8,128)(2,1)S(1)}, u32[]{:S(2)}, u32[]{:S(2)}) %collective-permute-start.3) | collective-permute-done | bytes 327712 | tf_op jit(solution)/shard_map/ppermute | solution.py:22
  12.8 0.0 collective-permute-start.4
  12.8 7.0 %collective-permute-done.5.refs_0_ = bf16[320,512]{1,0:T(8,128)(2,1)S(1)} collective-permute-done((bf16[320,512]{1,0:T(8,128)(2,1)S(1)}, bf16[320,512]{1,0:T(8,128)(2,1)S(1)}, u32[]{:S(2)}, u32[]{:S(2)}) %collective-permute-start.5) | collective-permute-done | bytes 327712 | tf_op jit(solution)/shard_map/ppermute | solution.py:22
  19.8 0.0 collective-permute-start.6
  19.8 0.8 %slice.3 = bf16[64,512]{1,0:T(8,128)(2,1)S(1)} slice(bf16[1024,512]{1,0:T(8,128)(2,1)} %tokens.3), slice={[0:64], [0:512]} | slice | bytes 131072 | tf_op jit(solution)/shard_map/slice | solution.py:262
  20.7 2.0 %collective-permute-start = (bf16[64,512]{1,0:T(8,128)(2,1)S(1)}, bf16[64,512]{1,0:T(8,128)(2,1)S(1)}, u32[]{:S(2)}, u32[]{:S(2)}) collective-permute-start(bf16[64,512]{1,0:T(8,128)(2,1)S(1)} %slice.3), channel_id=1, source_target_pairs={{0,2},{1,3},{2,0},{3,1},{4,6},{5,7},{6,4},{7,5},{8,10},{9,11},{10,... | collective-permute-start | bytes 196616 | tf_op jit(solution)/shard_map/ppermute | solution.py:22
  22.7 2.8 %collective-permute-done.refs_0_ = bf16[64,512]{1,0:T(8,128)(2,1)S(1)} collective-permute-done((bf16[64,512]{1,0:T(8,128)(2,1)S(1)}, bf16[64,512]{1,0:T(8,128)(2,1)S(1)}, u32[]{:S(2)}, u32[]{:S(2)}) %collective-permute-start) | collective-permute-done | bytes 65568 | tf_op jit(solution)/shard_map/ppermute | solution.py:22
  25.5 1.7 %collective-permute-start.9 = (bf16[128,512]{1,0:T(8,128)(2,1)S(1)}, bf16[128,512]{1,0:T(8,128)(2,1)S(1)}, u32[]{:S(2)}, u32[]{:S(2)}) collective-permute-start(bf16[128,512]{1,0:T(8,128)(2,1)S(1)} %get-tuple-element.77), channel_id=1, source_target_pairs={{0,2},{1,3},{2,0},{3,1},{4,6},{5,7},{6,4},{7,5},{8,10},{9,11},{10,... | collective-permute-start | bytes 393224 | tf_op jit(solution)/shard_map/ppermute | solution.py:22
  27.2 0.0 collective-permute-done.7.refs_0_
  27.2 0.0 collective-permute-start.8
  27.2 3.6 %collective-permute-done.9.refs_0_ = bf16[128,512]{1,0:T(8,128)(2,1)S(1)} collective-permute-done((bf16[128,512]{1,0:T(8,128)(2,1)S(1)}, bf16[128,512]{1,0:T(8,128)(2,1)S(1)}, u32[]{:S(2)}, u32[]{:S(2)}) %collective-permute-start.9) | collective-permute-done | bytes 131104 | tf_op jit(solution)/shard_map/ppermute | solution.py:22
  30.8 0.0 collective-permute-start.10
  30.8 0.0 collective-permute-done.2.refs_0_
  30.8 0.5 collective-permute-start.1
  31.3 3.6 %shard_map.73 = (bf16[2048,512]{1,0:T(8,128)(2,1)S(1)}, bf16[2048,512]{1,0:T(8,128)(2,1)S(1)}, bf16[2048,512]{1,0:T(8,128)(2,1)S(1)}, f32[1024,512]{1,0:T(8,128)...) custom-call(bf16[1024,512]{1,0:T(8,128)(2,1)} %tokens.3, bf16[2048,512]{1,0:T(8,128)(2,1)} %refs_0_.1, ...), custom_call_target="tpu_custom_call" | custom-call | tf_op jit(solution)/shard_map/pallas_call | solution.py:35
  34.9 1.8 %shard_map.74 = (f32[1024,512]{1,0:T(8,128)S(1)}, f32[1024,512]{1,0:T(8,128)S(1)}, f32[1024,512]{1,0:T(8,128)S(1)}) custom-call(bf16[1024,512]{1,0:T(8,128)(2,1)S(1)} %collective-permute-done.2.refs_0_, bf16[2048,512]{1,0:T(8,128)(2,1)S(1)} %get-tuple-element.50.refs_1_.refs_2_, bf16[2048,512]{1,0:T(8,128)(2,1)S(1)} %get-tuple-element.51.refs_2_, ...), custom_call_target="tpu_custom_call" | custom-call | tf_op jit(solution)/shard_map/pallas_call | solution.py:35
  36.7 0.0 collective-permute-done.1.refs_1_
  36.7 1.3 %shard_map.75 = (bf16[64,512]{1,0:T(8,128)(2,1)S(1)}, bf16[64,512]{1,0:T(8,128)(2,1)S(1)}, f32[4,128,128]{2,1,0:T(8,128)S(1)}, bf16[4,128,128]{2,1,0:T(8,128)(2,1)}) custom-call(bf16[64,512]{1,0:T(8,128)(2,1)S(1)} %collective-permute-done.refs_0_, bf16[64,512]{1,0:T(8,128)(2,1)S(1)} %collective-permute-done.1.refs_1_, ...), custom_call_target="tpu_custom_call" | custom-call | tf_op jit(solution)/shard_map/pallas_call | solution.py:35
  38.0 0.0 collective-permute-done.4.refs_1_
  38.1 1.7 %shard_map.79 = (bf16[320,512]{1,0:T(8,128)(2,1)S(1)}, bf16[320,512]{1,0:T(8,128)(2,1)S(1)}, f32[4,128,128]{2,1,0:T(8,128)S(1)}, bf16[4,128,128]{2,1,0:T(8,128)(2,1)}) custom-call(bf16[320,512]{1,0:T(8,128)(2,1)S(1)} %collective-permute-done.3.refs_0_, bf16[320,512]{1,0:T(8,128)(2,1)S(1)} %collective-permute-done.4.refs_1_, ...), custom_call_target="tpu_custom_call" | custom-call | tf_op jit(solution)/shard_map/pallas_call | solution.py:35
  39.8 0.0 collective-permute-done.6.refs_1_
  39.8 1.7 %shard_map.81 = (bf16[320,512]{1,0:T(8,128)(2,1)S(1)}, bf16[320,512]{1,0:T(8,128)(2,1)S(1)}, f32[4,128,128]{2,1,0:T(8,128)S(1)}, bf16[4,128,128]{2,1,0:T(8,128)(2,1)}) custom-call(bf16[320,512]{1,0:T(8,128)(2,1)S(1)} %collective-permute-done.5.refs_0_, bf16[320,512]{1,0:T(8,128)(2,1)S(1)} %collective-permute-done.6.refs_1_, ...), custom_call_target="tpu_custom_call" | custom-call | tf_op jit(solution)/shard_map/pallas_call | solution.py:35
  41.5 0.0 collective-permute-done.8.refs_1_
  41.5 1.4 %shard_map.83 = (bf16[192,512]{1,0:T(8,128)(2,1)S(1)}, bf16[192,512]{1,0:T(8,128)(2,1)S(1)}, f32[4,128,128]{2,1,0:T(8,128)S(1)}, bf16[4,128,128]{2,1,0:T(8,128)(2,1)}) custom-call(bf16[192,512]{1,0:T(8,128)(2,1)S(1)} %collective-permute-done.7.refs_0_, bf16[192,512]{1,0:T(8,128)(2,1)S(1)} %collective-permute-done.8.refs_1_, ...), custom_call_target="tpu_custom_call" | custom-call | tf_op jit(solution)/shard_map/pallas_call | solution.py:35
  43.0 0.0 collective-permute-done.10.refs_1_
  43.0 0.6 shard_map.85
  43.6 1.6 %collective-permute-start.11 = (bf16[4,128,128]{2,1,0:T(8,128)(2,1)S(1)}, bf16[4,128,128]{2,1,0:T(8,128)(2,1)S(1)}, u32[]{:S(2)}, u32[]{:S(2)}) collective-permute-start(bf16[4,128,128]{2,1,0:T(8,128)(2,1)S(1)} %get-tuple-element.92), channel_id=1, source_target_pairs={{0,4},{4,0},{8,12},{12,8},{1,5},{5,1},{9,13},{13,9},{2,6},{6,2},{1... | collective-permute-start | bytes 393224 | tf_op jit(solution)/shard_map/ppermute | solution.py:22
  45.2 3.8 %collective-permute-done.11.refs_10_.partner = bf16[4,128,128]{2,1,0:T(8,128)(2,1)S(1)} collective-permute-done((bf16[4,128,128]{2,1,0:T(8,128)(2,1)S(1)}, bf16[4,128,128]{2,1,0:T(8,128)(2,1)S(1)}, u32[]{:S(2)}, u32[]{:S(2)}) %collective-permute-start.11) | collective-permute-done | bytes 131104 | tf_op jit(solution)/shard_map/ppermute | solution.py:22
  49.1 2.6 %collective-permute-start.14 = (bf16[4,128,128]{2,1,0:T(8,128)(2,1)S(1)}, bf16[4,128,128]{2,1,0:T(8,128)(2,1)S(1)}, u32[]{:S(2)}, u32[]{:S(2)}) collective-permute-start(bf16[4,128,128]{2,1,0:T(8,128)(2,1)S(1)} %shard_map.88), channel_id=1, source_target_pairs={{0,8},{4,12},{8,0},{12,4},{1,9},{5,13},{9,1},{13,5},{2,10},{6,14},... | collective-permute-start | bytes 393224 | tf_op jit(solution)/shard_map/ppermute | solution.py:22
  51.7 1.6 %collective-permute-start.12 = (bf16[16,128]{1,0:T(8,128)(2,1)S(1)}, bf16[16,128]{1,0:T(8,128)(2,1)S(1)}, u32[]{:S(2)}, u32[]{:S(2)}) collective-permute-start(bf16[16,128]{1,0:T(8,128)(2,1)S(1)} %get-tuple-element.93), channel_id=1, source_target_pairs={{0,4},{4,0},{8,12},{12,8},{1,5},{5,1},{9,13},{13,9},{2,6},{6,2},{1... | collective-permute-start | bytes 12296 | tf_op jit(solution)/shard_map/ppermute | solution.py:22
  53.3 0.3 collective-permute-start.13
  53.7 0.2 shard_map.76.refs_7_
  53.8 1.1 %shard_map.86 = (f32[128,512]{1,0:T(8,128)S(1)}, bf16[128,512]{1,0:T(8,128)(2,1)S(1)}, bf16[128,512]{1,0:T(8,128)(2,1)S(1)}) custom-call(bf16[128,512]{1,0:T(8,128)(2,1)S(1)} %collective-permute-done.9.refs_0_, bf16[128,512]{1,0:T(8,128)(2,1)S(1)} %collective-permute-done.10.refs_1_, bf16[2048,512]{1,0:T(8,128)(2,1)S(1)} %get-tuple-element.50.refs_1_.refs_2_, ...), custom_call_target="tpu_custom_call" | custom-call | tf_op jit(solution)/shard_map/pallas_call | solution.py:35
  55.0 1.6 %shard_map.84 = (f32[192,512]{1,0:T(8,128)S(1)}, bf16[192,512]{1,0:T(8,128)(2,1)S(1)}, bf16[192,512]{1,0:T(8,128)(2,1)S(1)}) custom-call(bf16[192,512]{1,0:T(8,128)(2,1)S(1)} %collective-permute-done.7.refs_0_, bf16[192,512]{1,0:T(8,128)(2,1)S(1)} %collective-permute-done.8.refs_1_, bf16[2048,512]{1,0:T(8,128)(2,1)S(1)} %get-tuple-element.50.refs_1_.refs_2_, ...), custom_call_target="tpu_custom_call" | custom-call | tf_op jit(solution)/shard_map/pallas_call | solution.py:35
  56.6 2.0 %shard_map.82 = (f32[320,512]{1,0:T(8,128)S(1)}, bf16[320,512]{1,0:T(8,128)(2,1)S(1)}, bf16[320,512]{1,0:T(8,128)(2,1)S(1)}) custom-call(bf16[320,512]{1,0:T(8,128)(2,1)S(1)} %collective-permute-done.5.refs_0_, bf16[320,512]{1,0:T(8,128)(2,1)S(1)} %collective-permute-done.6.refs_1_, bf16[2048,512]{1,0:T(8,128)(2,1)S(1)} %get-tuple-element.50.refs_1_.refs_2_, ...), custom_call_target="tpu_custom_call" | custom-call | tf_op jit(solution)/shard_map/pallas_call | solution.py:35
  58.5 2.1 %shard_map.80 = (f32[320,512]{1,0:T(8,128)S(1)}, bf16[320,512]{1,0:T(8,128)(2,1)S(1)}, bf16[320,512]{1,0:T(8,128)(2,1)S(1)}) custom-call(bf16[320,512]{1,0:T(8,128)(2,1)S(1)} %collective-permute-done.3.refs_0_, bf16[320,512]{1,0:T(8,128)(2,1)S(1)} %collective-permute-done.4.refs_1_, bf16[2048,512]{1,0:T(8,128)(2,1)S(1)} %get-tuple-element.50.refs_1_.refs_2_, ...), custom_call_target="tpu_custom_call" | custom-call | tf_op jit(solution)/shard_map/pallas_call | solution.py:35
  60.6 0.9 %shard_map.77 = (f32[64,512]{1,0:T(8,128)S(1)}, bf16[64,512]{1,0:T(8,128)(2,1)S(1)}, bf16[64,512]{1,0:T(8,128)(2,1)S(1)}) custom-call(bf16[64,512]{1,0:T(8,128)(2,1)S(1)} %collective-permute-done.refs_0_, bf16[64,512]{1,0:T(8,128)(2,1)S(1)} %collective-permute-done.1.refs_1_, bf16[2048,512]{1,0:T(8,128)(2,1)S(1)} %get-tuple-element.50.refs_1_.refs_2_, ...), custom_call_target="tpu_custom_call" | custom-call | tf_op jit(solution)/shard_map/pallas_call | solution.py:35
  61.5 0.0 collective-permute-done.13.refs_12_
  61.5 0.0 copy-start.1
  61.5 0.4 shard_map.87.refs_5_
  62.0 0.0 collective-permute-done.14.refs_6_
  62.0 0.2 copy-done.1
  62.2 1.6 %shard_map.89 = bf16[1024,512]{1,0:T(8,128)(2,1)} custom-call(bf16[64,512]{1,0:T(8,128)(2,1)S(1)} %get-tuple-element.61.refs_0_, bf16[320,512]{1,0:T(8,128)(2,1)S(1)} %get-tuple-element.66.refs_1_, bf16[320,512]{1,0:T(8,128)(2,1)S(1)} %get-tuple-element.71.refs_2_, bf16[192,512]{1,0:T(8,128)(2,1)S(1)} %get-tuple-element.76.refs_3_, ...), custom_call_target="tpu_custom_call" | custom-call | tf_op jit(solution)/shard_map/pallas_call | solution.py:35
  (6 shorter events, 0.0 us)
Async XLA Ops:
  0.0 30.8 %collective-permute-start.2 = (bf16[1024,512]{1,0:T(8,128)(2,1)}, bf16[1024,512]{1,0:T(8,128)(2,1)S(1)}, u32[]{:S(2)}, u32[]{:S(2)}) collective-permute-start(bf16[1024,512]{1,0:T(8,128)(2,1)} %tokens.3), channel_id=1, source_target_pairs={{0,1},{1,0},{2,3},{3,2},{4,5},{5,4},{6,7},{7,6},{8,9},{9,8},{10,11... | collective-permute-start | bytes 3145736 | tf_op jit(solution)/shard_map/ppermute | solution.py:22
  1.7 11.1 %collective-permute-start.3 = (bf16[320,512]{1,0:T(8,128)(2,1)S(1)}, bf16[320,512]{1,0:T(8,128)(2,1)S(1)}, u32[]{:S(2)}, u32[]{:S(2)}) collective-permute-start(bf16[320,512]{1,0:T(8,128)(2,1)S(1)} %get-tuple-element.62), channel_id=1, source_target_pairs={{0,2},{1,3},{2,0},{3,1},{4,6},{5,7},{6,4},{7,5},{8,10},{9,11},{10,... | collective-permute-start | bytes 983048 | tf_op jit(solution)/shard_map/ppermute | solution.py:22
  4.2 15.6 %collective-permute-start.5 = (bf16[320,512]{1,0:T(8,128)(2,1)S(1)}, bf16[320,512]{1,0:T(8,128)(2,1)S(1)}, u32[]{:S(2)}, u32[]{:S(2)}) collective-permute-start(bf16[320,512]{1,0:T(8,128)(2,1)S(1)} %get-tuple-element.67), channel_id=1, source_target_pairs={{0,2},{1,3},{2,0},{3,1},{4,6},{5,7},{6,4},{7,5},{8,10},{9,11},{10,... | collective-permute-start | bytes 983048 | tf_op jit(solution)/shard_map/ppermute | solution.py:22
  4.3 22.9 %collective-permute-start.7 = (bf16[192,512]{1,0:T(8,128)(2,1)S(1)}, bf16[192,512]{1,0:T(8,128)(2,1)S(1)}, u32[]{:S(2)}, u32[]{:S(2)}) collective-permute-start(bf16[192,512]{1,0:T(8,128)(2,1)S(1)} %get-tuple-element.72), channel_id=1, source_target_pairs={{0,2},{1,3},{2,0},{3,1},{4,6},{5,7},{6,4},{7,5},{8,10},{9,11},{10,... | collective-permute-start | bytes 589832 | tf_op jit(solution)/shard_map/ppermute | solution.py:22
  12.8 25.2 %collective-permute-start.4 = (bf16[320,512]{1,0:T(8,128)(2,1)S(1)}, bf16[320,512]{1,0:T(8,128)(2,1)S(1)}, u32[]{:S(2)}, u32[]{:S(2)}) collective-permute-start(bf16[320,512]{1,0:T(8,128)(2,1)S(1)} %collective-permute-done.3.refs_0_), channel_id=1, source_target_pairs={{0,1},{1,0},{2,3},{3,2},{4,5},{5,4},{6,7},{7,6},{8,9},{9,8},{10,11... | collective-permute-start | bytes 983048 | tf_op jit(solution)/shard_map/ppermute | solution.py:22
  19.8 19.9 %collective-permute-start.6 = (bf16[320,512]{1,0:T(8,128)(2,1)S(1)}, bf16[320,512]{1,0:T(8,128)(2,1)S(1)}, u32[]{:S(2)}, u32[]{:S(2)}) collective-permute-start(bf16[320,512]{1,0:T(8,128)(2,1)S(1)} %collective-permute-done.5.refs_0_), channel_id=1, source_target_pairs={{0,1},{1,0},{2,3},{3,2},{4,5},{5,4},{6,7},{7,6},{8,9},{9,8},{10,11... | collective-permute-start | bytes 983048 | tf_op jit(solution)/shard_map/ppermute | solution.py:22
  20.7 4.8 %collective-permute-start = (bf16[64,512]{1,0:T(8,128)(2,1)S(1)}, bf16[64,512]{1,0:T(8,128)(2,1)S(1)}, u32[]{:S(2)}, u32[]{:S(2)}) collective-permute-start(bf16[64,512]{1,0:T(8,128)(2,1)S(1)} %slice.3), channel_id=1, source_target_pairs={{0,2},{1,3},{2,0},{3,1},{4,6},{5,7},{6,4},{7,5},{8,10},{9,11},{10,... | collective-permute-start | bytes 196616 | tf_op jit(solution)/shard_map/ppermute | solution.py:22
  25.5 5.3 %collective-permute-start.9 = (bf16[128,512]{1,0:T(8,128)(2,1)S(1)}, bf16[128,512]{1,0:T(8,128)(2,1)S(1)}, u32[]{:S(2)}, u32[]{:S(2)}) collective-permute-start(bf16[128,512]{1,0:T(8,128)(2,1)S(1)} %get-tuple-element.77), channel_id=1, source_target_pairs={{0,2},{1,3},{2,0},{3,1},{4,6},{5,7},{6,4},{7,5},{8,10},{9,11},{10,... | collective-permute-start | bytes 393224 | tf_op jit(solution)/shard_map/ppermute | solution.py:22
  27.2 14.3 %collective-permute-start.8 = (bf16[192,512]{1,0:T(8,128)(2,1)S(1)}, bf16[192,512]{1,0:T(8,128)(2,1)S(1)}, u32[]{:S(2)}, u32[]{:S(2)}) collective-permute-start(bf16[192,512]{1,0:T(8,128)(2,1)S(1)} %collective-permute-done.7.refs_0_), channel_id=1, source_target_pairs={{0,1},{1,0},{2,3},{3,2},{4,5},{5,4},{6,7},{7,6},{8,9},{9,8},{10,11... | collective-permute-start | bytes 589832 | tf_op jit(solution)/shard_map/ppermute | solution.py:22
  30.8 12.2 %collective-permute-start.10 = (bf16[128,512]{1,0:T(8,128)(2,1)S(1)}, bf16[128,512]{1,0:T(8,128)(2,1)S(1)}, u32[]{:S(2)}, u32[]{:S(2)}) collective-permute-start(bf16[128,512]{1,0:T(8,128)(2,1)S(1)} %collective-permute-done.9.refs_0_), channel_id=1, source_target_pairs={{0,1},{1,0},{2,3},{3,2},{4,5},{5,4},{6,7},{7,6},{8,9},{9,8},{10,11... | collective-permute-start | bytes 393224 | tf_op jit(solution)/shard_map/ppermute | solution.py:22
  30.8 5.9 %collective-permute-start.1 = (bf16[64,512]{1,0:T(8,128)(2,1)S(1)}, bf16[64,512]{1,0:T(8,128)(2,1)S(1)}, u32[]{:S(2)}, u32[]{:S(2)}) collective-permute-start(bf16[64,512]{1,0:T(8,128)(2,1)S(1)} %collective-permute-done.refs_0_), channel_id=1, source_target_pairs={{0,1},{1,0},{2,3},{3,2},{4,5},{5,4},{6,7},{7,6},{8,9},{9,8},{10,11... | collective-permute-start | bytes 196616 | tf_op jit(solution)/shard_map/ppermute | solution.py:22
  43.0 10.7 %copy-start.2 = (f32[4,16]{1,0:T(4,128)S(1)}, f32[4,16]{1,0:T(4,128)}, u32[]{:S(2)}) copy-start(f32[4,16]{1,0:T(4,128)} %table.1) | copy-start | bytes 772
  43.0 10.9 %copy-start = (s32[6,1024]{1,0:T(8,128)S(1)}, s32[6,1024]{1,0:T(8,128)}, u32[]{:S(2)}) copy-start(s32[6,1024]{1,0:T(8,128)} %refs_6_.9) | copy-start | bytes 73732
  43.6 5.5 %collective-permute-start.11 = (bf16[4,128,128]{2,1,0:T(8,128)(2,1)S(1)}, bf16[4,128,128]{2,1,0:T(8,128)(2,1)S(1)}, u32[]{:S(2)}, u32[]{:S(2)}) collective-permute-start(bf16[4,128,128]{2,1,0:T(8,128)(2,1)S(1)} %get-tuple-element.92), channel_id=1, source_target_pairs={{0,4},{4,0},{8,12},{12,8},{1,5},{5,1},{9,13},{13,9},{2,6},{6,2},{1... | collective-permute-start | bytes 393224 | tf_op jit(solution)/shard_map/ppermute | solution.py:22
  49.1 12.9 %collective-permute-start.14 = (bf16[4,128,128]{2,1,0:T(8,128)(2,1)S(1)}, bf16[4,128,128]{2,1,0:T(8,128)(2,1)S(1)}, u32[]{:S(2)}, u32[]{:S(2)}) collective-permute-start(bf16[4,128,128]{2,1,0:T(8,128)(2,1)S(1)} %shard_map.88), channel_id=1, source_target_pairs={{0,8},{4,12},{8,0},{12,4},{1,9},{5,13},{9,1},{13,5},{2,10},{6,14},... | collective-permute-start | bytes 393224 | tf_op jit(solution)/shard_map/ppermute | solution.py:22
  51.7 9.7 %collective-permute-start.12 = (bf16[16,128]{1,0:T(8,128)(2,1)S(1)}, bf16[16,128]{1,0:T(8,128)(2,1)S(1)}, u32[]{:S(2)}, u32[]{:S(2)}) collective-permute-start(bf16[16,128]{1,0:T(8,128)(2,1)S(1)} %get-tuple-element.93), channel_id=1, source_target_pairs={{0,4},{4,0},{8,12},{12,8},{1,5},{5,1},{9,13},{13,9},{2,6},{6,2},{1... | collective-permute-start | bytes 12296 | tf_op jit(solution)/shard_map/ppermute | solution.py:22
  53.3 8.2 %collective-permute-start.13 = (bf16[16,128]{1,0:T(8,128)(2,1)S(1)}, bf16[16,128]{1,0:T(8,128)(2,1)S(1)}, u32[]{:S(2)}, u32[]{:S(2)}) collective-permute-start(bf16[16,128]{1,0:T(8,128)(2,1)S(1)} %get-tuple-element.93), channel_id=1, source_target_pairs={{0,8},{4,12},{8,0},{12,4},{1,9},{5,13},{9,1},{13,5},{2,10},{6,14},... | collective-permute-start | bytes 12296 | tf_op jit(solution)/shard_map/ppermute | solution.py:22
  61.5 0.7 %copy-start.1 = (f32[512]{0:T(512)S(1)}, f32[512]{0:T(512)}, u32[]{:S(2)}) copy-start(f32[512]{0:T(512)} %param.13) | copy-start | bytes 6148

commit v4 on v3

--- a/solution.py
+++ b/solution.py
@@ -8,7 +8,7 @@
 from jax.sharding import PartitionSpec as P
 
 
-CHUNKS = (1, 5, 5, 3, 2)
+CHUNKS = (3, 2, 2, 1)
 EPS = 1e-06
 F32 = jnp.float32
 BF16 = jnp.bfloat16
@@ -30,7 +30,7 @@
     return pltpu.with_memory_space_constraint(array, pltpu.HBM)
 
 
-def call(kernel, outs, in_specs, args, out_specs=None, scratch=(), limit=8):
+def call(kernel, outs, in_specs, args, out_specs=None, scratch=(), limit=8, aliases={}):
     kept = [pltpu.VMEM(*out) for out in outs]
     return pl.pallas_call(
         kernel,
@@ -38,6 +38,7 @@
         in_specs=in_specs,
         out_specs=out_specs or [VMEM] * len(outs),
         scratch_shapes=scratch,
+        input_output_aliases=aliases,
         compiler_params=pltpu.CompilerParams(vmem_limit_bytes=limit << 20),
     )(*args)
 
@@ -103,32 +104,33 @@
         grown[...] = acc
 
 
-def late_sum(base, pieces, weight, early, lo, rows):
+def late_sum(base, pieces, weight, early, lo, rows, cols):
     me = lax.axis_index("head")
     depth = pieces[0].shape[1]
-    acc = early[lo : lo + rows, :]
+    acc = early[lo : lo + rows, cols]
     for offset, piece in enumerate(pieces):
-        acc = acc + dot(piece[...], weight_rows(me, weight, base + offset, depth))
+        start = pl.multiple_of((me ^ (base + offset)) * depth, depth)
+        acc = acc + dot(piece[...], weight[pl.ds(start, depth), cols])
     return acc
 
 
-def kv_kernel(base, lo, heads, *refs):
+def kv_kernel(base, lo, size, first, *refs):
     pieces = refs[:base]
     k_weight, v_weight, k_early, v_early = refs[base : base + 4]
-    state_in = refs[base + 4] if lo else None
+    state_in = refs[base + 4 : -4]
     keys, values, state, state_low = refs[-4:]
     rows, width = keys.shape
-    size = width // heads
-    raw_k = late_sum(base, pieces, k_weight, k_early, lo, rows)
-    raw_v = late_sum(base, pieces, v_weight, v_early, lo, rows).astype(BF16)
+    mine = slice(first * size, first * size + width)
+    raw_k = late_sum(base, pieces, k_weight, k_early, lo, rows, mine)
+    raw_v = late_sum(base, pieces, v_weight, v_early, lo, rows, mine).astype(BF16)
     values[...] = raw_v
-    for head in range(heads):
+    for head in range(width // size):
         cols = slice(head * size, (head + 1) * size)
         key = unit_rows(raw_k[:, cols])
         keys[:, cols] = key
         total = dot(key, raw_v[:, cols], ((0,), (0,)))
-        if lo:
-            total = state_in[head] + total
+        if state_in:
+            total = state_in[0][first + head] + total
         state[head] = total
         state_low[head] = total.astype(BF16)
 
@@ -166,25 +168,29 @@
     return weigh(picked(0)), weigh(rest), far
 
 
-def query_kernel(base, lo, heads, depth, *refs):
+def query_kernel(base, groups, lo, heads, depth, *refs):
     pieces = refs[:base]
-    q_weight, q_early, keys, values, index, table = refs[base : base + 6]
-    state_in = refs[base + 6] if lo else None
+    q_weight, q_early, index, table = refs[base : base + 4]
+    keys = refs[base + 4 : base + 4 + groups]
+    values = refs[base + 4 + groups : base + 4 + 2 * groups]
+    state_in = refs[base + 4 + 2 * groups : -1 - depth]
     part = refs[-1 - depth]
     scaled = refs[-depth:]
-    rows, width = keys.shape
+    rows, width = part.shape
     size = width // heads
+    per = heads // groups
     own, rest, far = level_weights(depth, lax.axis_index("seq"), index[:, lo : lo + rows], table)
-    raw_q = late_sum(base, pieces, q_weight, q_early, lo, rows)
+    raw_q = late_sum(base, pieces, q_weight, q_early, lo, rows, slice(0, width))
     causal = lax.broadcasted_iota(jnp.int32, (rows, rows), 0) >= lax.broadcasted_iota(jnp.int32, (rows, rows), 1)
     for head in range(heads):
         cols = slice(head * size, (head + 1) * size)
         query = unit_rows(raw_q[:, cols])
-        scores = dot(query, keys[:, cols], ((1,), (1,)))
+        inside = slice(head % per * size, (head % per + 1) * size)
+        scores = dot(query, keys[head // per][:, inside], ((1,), (1,)))
         scores = jnp.where(causal, scores, 0.0).astype(BF16)
-        local = dot(scores, values[:, cols])
-        if lo:
-            local = local + dot(query, state_in[head].astype(BF16))
+        local = dot(scores, values[head // per][:, inside])
+        if state_in:
+            local = local + dot(query, state_in[0][head].astype(BF16))
         wide = query.astype(F32)
         empty = (wide * rest[:, cols]).astype(BF16)
         part[:, cols] = own[:, cols] * local + dot(empty, jnp.zeros((size, size), BF16))
@@ -198,38 +204,41 @@
         out[...] = summed.astype(out.dtype)
 
 
-def fold_kernel(heads, levels, edges, *refs):
+def fold_kernel(heads, groups, levels, edges, *refs):
     count = len(edges) - 1
     parts = refs[:count]
     scaled = [refs[count * (1 + level) : count * (2 + level)] for level in range(levels)]
-    merged = refs[count * (1 + levels) :][:levels]
+    merged = refs[count * (1 + levels) : -1]
     total = refs[-1]
     size = total.shape[1] // heads
+    per = heads // groups
     for i in range(count):
         rows = slice(edges[i], edges[i + 1])
         for head in range(heads):
             cols = slice(head * size, (head + 1) * size)
             acc = parts[i][:, cols]
             for level in range(levels):
-                acc = acc + dot(scaled[level][i][:, cols], merged[level][head])
+                acc = acc + dot(scaled[level][i][:, cols], merged[level * groups + head // per][head % per])
             total[rows, cols] = acc
 
 
-def final_kernel(heads, edges, *refs):
+def final_kernel(edges, first, *refs):
     count = len(edges) - 1
     scaled = refs[:count]
-    before, merged, gain, out, done, sems = refs[count:]
-    size = done.shape[1] // heads
+    before, merged, gain = refs[count : count + 3]
+    out, done, sems = refs[-3:]
+    per, size, _ = merged.shape
+    mine = slice(first * size, (first + per) * size)
     share = jnp.full((size, size), 1.0 / size, BF16)
     copies = []
     for i in range(count):
         rows = slice(edges[i], edges[i + 1])
-        for head in range(heads):
-            cols = slice(head * size, (head + 1) * size)
+        for head in range(per):
+            cols = slice((first + head) * size, (first + head + 1) * size)
             total = before[rows, cols] + dot(scaled[i][:, cols], merged[head])
             mean = dot((total * total).astype(BF16), share)
-            done[rows, cols] = (total * lax.rsqrt(mean + EPS) * gain[0:1, cols]).astype(BF16)
-        copy = pltpu.make_async_copy(done.at[rows], out.at[rows], sems.at[i])
+            done[rows, head * size : (head + 1) * size] = (total * lax.rsqrt(mean + EPS) * gain[0:1, cols]).astype(BF16)
+        copy = pltpu.make_async_copy(done.at[rows], out.at[rows, mine], sems.at[i])
         copy.start()
         copies.append(copy)
     for copy in copies:
@@ -258,18 +267,17 @@
     for share in CHUNKS:
         edges.append(edges[-1] + share * unit)
     spans = list(zip(edges[:-1], edges[1:]))
+    last = len(spans) - 1
 
     cuts = [tokens[: spans[0][1]]]
-    boxes = [(lo, hi, feat_here) for lo, hi in spans[1:]] + [(0, 16, 128)]
-    *rest, small = call(
+    boxes = [(lo, hi, feat_here) for lo, hi in spans[1:]]
+    cuts += call(
         functools.partial(cut_kernel, boxes),
         [((hi - lo, wide), BF16) for lo, hi, wide in boxes],
         [HBM],
         (outside(tokens),),
         scratch=[pltpu.SemaphoreType.DMA((len(boxes),))],
     )
-    cuts += rest
-    greetings = [swap(small, "seq", 1 << level) for level in range(depth)]
     far = [swap(piece, "head", base) for piece in cuts]
     near = hop(tokens, base)[1:]
 
@@ -290,54 +298,70 @@
     )
     table = call(table_kernel, [((2 * quant, width), BF16)], [VMEM], (level_table,))[0]
 
+    split = 2 - heads % 2
+    per = heads // split
     state = []
     parts = []
     scaled = []
     for i, (lo, hi) in enumerate(spans):
         rows = hi - lo
         pieces = hop(far[i], base)
-        before = state
-        args = (*pieces, k_weight, v_weight, early[1], early[2], *before)
-        keys, values, total, low = call(
-            functools.partial(kv_kernel, base, lo, heads),
-            [((rows, width), BF16)] * 2 + [((heads, size, size), F32), ((heads, size, size), BF16)],
-            [VMEM] * len(args),
-            args,
-        )
-        state = [total]
-        args = (*pieces, q_weight, early[0], keys, values, level_index, table, *before)
+        groups = split if i == last else 1
+        keys, values, totals, lows = [], [], [], []
+        for group in range(groups):
+            count = heads // groups
+            args = (*pieces, k_weight, v_weight, early[1], early[2], *state)
+            results = call(
+                functools.partial(kv_kernel, base, lo, size, group * count),
+                [((rows, count * size), BF16)] * 2 + [((count, size, size), F32), ((count, size, size), BF16)],
+                [VMEM] * len(args),
+                args,
+            )
+            for items, result in zip((keys, values, totals, lows), results):
+                items.append(result)
+        args = (*pieces, q_weight, early[0], level_index, table, *keys, *values, *state)
         outs = call(
-            functools.partial(query_kernel, base, lo, heads, depth),
+            functools.partial(query_kernel, base, groups, lo, heads, depth),
             [((rows, width), F32)] + [((rows, width), BF16)] * depth,
             [VMEM] * len(args),
             args,
         )
         parts.append(outs[0])
         scaled.append(outs[1:])
+        state = totals
 
     merged = []
     for level in range(depth):
-        partner = swap(low, "seq", 1 << level)
-        merged.append(partner)
+        partners = [swap(low, "seq", 1 << level) for low in lows]
+        merged.append(partners)
         if level + 1 < depth:
-            shape = (heads, size, size)
+            shape = (per, size, size)
             kinds = [(shape, BF16)] + [(shape, F32)] * (level + 2 < depth)
-            low, *rest = call(add_kernel, kinds, [VMEM, VMEM], (total, partner))
-            total = rest[0] if rest else None
-
-    inputs = parts + [chunk[level] for level in range(depth - 1) for chunk in scaled] + merged[:-1] + greetings
+            grown = [
+                call(add_kernel, kinds, [VMEM, VMEM], (total, partner))
+                for total, partner in zip(totals, partners)
+            ]
+            lows = [pair[0] for pair in grown]
+            totals = [pair[-1] for pair in grown]
+
+    inputs = parts + [chunk[level] for level in range(depth - 1) for chunk in scaled]
+    inputs += [partner for partners in merged[:-1] for partner in partners]
     before = call(
-        functools.partial(fold_kernel, heads, depth - 1, edges), [(big, F32)], [VMEM] * len(inputs), inputs
+        functools.partial(fold_kernel, heads, split, depth - 1, edges), [(big, F32)], [VMEM] * len(inputs), inputs
     )[0]
-    inputs = [chunk[-1] for chunk in scaled] + [before, merged[-1], out_gain.reshape(1, width)]
-    return call(
-        functools.partial(final_kernel, heads, edges),
-        [(big, BF16)],
-        [VMEM] * len(inputs),
-        inputs,
-        out_specs=[ANY],
-        scratch=[pltpu.VMEM(big, BF16), pltpu.SemaphoreType.DMA((len(spans),))],
-    )[0]
+    out = []
+    for group in range(split):
+        inputs = [chunk[-1] for chunk in scaled] + [before, merged[-1][group], out_gain.reshape(1, width)]
+        out = list(call(
+            functools.partial(final_kernel, edges, group * per),
+            [(big, BF16)],
+            [VMEM] * len(inputs) + [ANY] * len(out),
+            inputs + out,
+            out_specs=[ANY],
+            scratch=[pltpu.VMEM((row_count, per * size), BF16), pltpu.SemaphoreType.DMA((len(spans),))],
+            aliases={len(inputs): 0} if out else {},
+        ))
+    return out[0]
 
 
 def solution(mesh):

time: 63.9 us -> 61.3 us (0.959)
  starting transfers between devices: 15.5 us -> 13.8 us
  Pallas kernels: 23.3 us -> 21.9 us
    ppermute x15 -> x13, starting transfers between devices: 15.5 us -> 13.8 us  [swap(): return lax.ppermute(block, axis, route)]
    pallas_call x17 -> x18, Pallas kernels: 23.3 us -> 21.9 us  [call(): pl.pallas_call(kernel, out_shape=kept if out_specs is None else [jax.Shap...]
    ppermute x15 -> x13, waiting for transfers between devices: 23.8 us -> 23.9 us  [swap(): return lax.ppermute(block, axis, route)]
  transfers between devices with their start and end apart: 15 -> 13, of which waited for: 5 -> 5; matrix products, arithmetic and copies ran while one was open for 1% -> 2% of each run, Pallas kernels for 33% -> 33%
where the time goes in v4:
time: 61.3 us; the launch traced here: 61.1 us
  waiting for transfers between devices  23.9 us (39%)
  Pallas kernels  21.9 us (36%)
  starting transfers between devices  13.8 us (23%)
  local copies, waits for them, and re-layouts  1.27 us (2%)
    ppermute x13, waiting for transfers between devices, swap(): return lax.ppermute(block, axis, route)  23.9 us
    pallas_call x18, Pallas kernels, call(): pl.pallas_call(kernel, out_shape=kept if out_specs is None else [jax.Shap...  21.9 us
    ppermute x13, starting transfers between devices, swap(): return lax.ppermute(block, axis, route)  13.8 us
  transfers between devices with their start and end apart: 13, of which 5 were waited for; matrix products, arithmetic and copies ran while one was open for 2% of the time, Pallas kernels for 33%

profile of v4, /device:TPU:0, one launch (start us, length us, event | category | flops | bytes accessed | tf_op | source)
XLA Modules:
  0.0 61.1 jit_solution(17273242280999226437)
XLA Ops:
  0.0 0.5 collective-permute-start.2
  0.5 1.0 %slice.3 = bf16[384,512]{1,0:T(8,128)(2,1)S(1)} slice(bf16[1024,512]{1,0:T(8,128)(2,1)} %tokens.3), slice={[0:384], [0:512]} | slice | bytes 786432 | tf_op jit(solution)/shard_map/slice | solution.py:272
  1.5 2.5 %collective-permute-start = (bf16[384,512]{1,0:T(8,128)(2,1)S(1)}, bf16[384,512]{1,0:T(8,128)(2,1)S(1)}, u32[]{:S(2)}, u32[]{:S(2)}) collective-permute-start(bf16[384,512]{1,0:T(8,128)(2,1)S(1)} %slice.3), channel_id=1, source_target_pairs={{0,2},{1,3},{2,0},{3,1},{4,6},{5,7},{6,4},{7,5},{8,10},{9,11},{10,... | collective-permute-start | bytes 1179656 | tf_op jit(solution)/shard_map/ppermute | solution.py:22
  4.1 1.1 %shard_map.78 = (bf16[256,512]{1,0:T(8,128)(2,1)S(1)}, bf16[256,512]{1,0:T(8,128)(2,1)S(1)}, bf16[128,512]{1,0:T(8,128)(2,1)S(1)}) custom-call(bf16[1024,512]{1,0:T(8,128)(2,1)} %tokens.3), custom_call_target="tpu_custom_call" | custom-call | tf_op jit(solution)/shard_map/pallas_call | solution.py:35
  5.2 0.1 collective-permute-start.3
  5.2 2.0 %collective-permute-start.5 = (bf16[256,512]{1,0:T(8,128)(2,1)S(1)}, bf16[256,512]{1,0:T(8,128)(2,1)S(1)}, u32[]{:S(2)}, u32[]{:S(2)}) collective-permute-start(bf16[256,512]{1,0:T(8,128)(2,1)S(1)} %get-tuple-element.63), channel_id=1, source_target_pairs={{0,2},{1,3},{2,0},{3,1},{4,6},{5,7},{6,4},{7,5},{8,10},{9,11},{10,... | collective-permute-start | bytes 786440 | tf_op jit(solution)/shard_map/ppermute | solution.py:22
  7.2 6.8 %collective-permute-done.refs_0_ = bf16[384,512]{1,0:T(8,128)(2,1)S(1)} collective-permute-done((bf16[384,512]{1,0:T(8,128)(2,1)S(1)}, bf16[384,512]{1,0:T(8,128)(2,1)S(1)}, u32[]{:S(2)}, u32[]{:S(2)}) %collective-permute-start) | collective-permute-done | bytes 393248 | tf_op jit(solution)/shard_map/ppermute | solution.py:22
  14.0 0.0 collective-permute-start.1
  14.0 5.6 %collective-permute-done.3.refs_0_ = bf16[256,512]{1,0:T(8,128)(2,1)S(1)} collective-permute-done((bf16[256,512]{1,0:T(8,128)(2,1)S(1)}, bf16[256,512]{1,0:T(8,128)(2,1)S(1)}, u32[]{:S(2)}, u32[]{:S(2)}) %collective-permute-start.3) | collective-permute-done | bytes 262176 | tf_op jit(solution)/shard_map/ppermute | solution.py:22
  19.6 0.0 collective-permute-start.4
  19.6 5.4 %collective-permute-done.5.refs_0_ = bf16[256,512]{1,0:T(8,128)(2,1)S(1)} collective-permute-done((bf16[256,512]{1,0:T(8,128)(2,1)S(1)}, bf16[256,512]{1,0:T(8,128)(2,1)S(1)}, u32[]{:S(2)}, u32[]{:S(2)}) %collective-permute-start.5) | collective-permute-done | bytes 262176 | tf_op jit(solution)/shard_map/ppermute | solution.py:22
  25.1 0.0 collective-permute-start.6
  25.1 1.7 %collective-permute-start.7 = (bf16[128,512]{1,0:T(8,128)(2,1)S(1)}, bf16[128,512]{1,0:T(8,128)(2,1)S(1)}, u32[]{:S(2)}, u32[]{:S(2)}) collective-permute-start(bf16[128,512]{1,0:T(8,128)(2,1)S(1)} %get-tuple-element.68), channel_id=1, source_target_pairs={{0,2},{1,3},{2,0},{3,1},{4,6},{5,7},{6,4},{7,5},{8,10},{9,11},{10,... | collective-permute-start | bytes 393224 | tf_op jit(solution)/shard_map/ppermute | solution.py:22
  26.8 4.2 %collective-permute-done.7.refs_0_ = bf16[128,512]{1,0:T(8,128)(2,1)S(1)} collective-permute-done((bf16[128,512]{1,0:T(8,128)(2,1)S(1)}, bf16[128,512]{1,0:T(8,128)(2,1)S(1)}, u32[]{:S(2)}, u32[]{:S(2)}) %collective-permute-start.7) | collective-permute-done | bytes 131104 | tf_op jit(solution)/shard_map/ppermute | solution.py:22
  31.0 0.0 collective-permute-start.8
  31.0 3.6 %shard_map.73 = (bf16[2048,512]{1,0:T(8,128)(2,1)S(1)}, bf16[2048,512]{1,0:T(8,128)(2,1)S(1)}, bf16[2048,512]{1,0:T(8,128)(2,1)S(1)}, f32[1024,512]{1,0:T(8,128)...) custom-call(bf16[1024,512]{1,0:T(8,128)(2,1)} %tokens.3, bf16[2048,512]{1,0:T(8,128)(2,1)} %refs_0_.1, ...), custom_call_target="tpu_custom_call" | custom-call | tf_op jit(solution)/shard_map/pallas_call | solution.py:35
  34.6 0.0 collective-permute-done.2.refs_0_
  34.6 1.8 %shard_map.74 = (f32[1024,512]{1,0:T(8,128)S(1)}, f32[1024,512]{1,0:T(8,128)S(1)}, f32[1024,512]{1,0:T(8,128)S(1)}) custom-call(bf16[1024,512]{1,0:T(8,128)(2,1)S(1)} %collective-permute-done.2.refs_0_, bf16[2048,512]{1,0:T(8,128)(2,1)S(1)} %get-tuple-element.46.refs_1_.refs_2_, bf16[2048,512]{1,0:T(8,128)(2,1)S(1)} %get-tuple-element.47.refs_2_, ...), custom_call_target="tpu_custom_call" | custom-call | tf_op jit(solution)/shard_map/pallas_call | solution.py:35
  36.4 0.0 collective-permute-done.1.refs_1_
  36.4 1.9 %shard_map.76 = (bf16[384,512]{1,0:T(8,128)(2,1)S(1)}, bf16[384,512]{1,0:T(8,128)(2,1)S(1)}, f32[4,128,128]{2,1,0:T(8,128)S(1)}, bf16[4,128,128]{2,1,0:T(8,128)(2,1)}) custom-call(bf16[384,512]{1,0:T(8,128)(2,1)S(1)} %collective-permute-done.refs_0_, bf16[384,512]{1,0:T(8,128)(2,1)S(1)} %collective-permute-done.1.refs_1_, ...), custom_call_target="tpu_custom_call" | custom-call | tf_op jit(solution)/shard_map/pallas_call | solution.py:35
  38.3 0.0 collective-permute-done.4.refs_1_
  38.3 1.6 %shard_map.79 = (bf16[256,512]{1,0:T(8,128)(2,1)S(1)}, bf16[256,512]{1,0:T(8,128)(2,1)S(1)}, f32[4,128,128]{2,1,0:T(8,128)S(1)}, bf16[4,128,128]{2,1,0:T(8,128)(2,1)}) custom-call(bf16[256,512]{1,0:T(8,128)(2,1)S(1)} %collective-permute-done.3.refs_0_, bf16[256,512]{1,0:T(8,128)(2,1)S(1)} %collective-permute-done.4.refs_1_, ...), custom_call_target="tpu_custom_call" | custom-call | tf_op jit(solution)/shard_map/pallas_call | solution.py:35
  39.9 0.0 collective-permute-done.6.refs_1_
  39.9 1.6 %shard_map.81 = (bf16[256,512]{1,0:T(8,128)(2,1)S(1)}, bf16[256,512]{1,0:T(8,128)(2,1)S(1)}, f32[4,128,128]{2,1,0:T(8,128)S(1)}, bf16[4,128,128]{2,1,0:T(8,128)(2,1)}) custom-call(bf16[256,512]{1,0:T(8,128)(2,1)S(1)} %collective-permute-done.5.refs_0_, bf16[256,512]{1,0:T(8,128)(2,1)S(1)} %collective-permute-done.6.refs_1_, ...), custom_call_target="tpu_custom_call" | custom-call | tf_op jit(solution)/shard_map/pallas_call | solution.py:35
  41.5 0.0 collective-permute-done.8.refs_1_
  41.5 0.6 shard_map.83
  42.1 0.0 copy-start
  42.1 1.9 %collective-permute-start.9 = (bf16[2,128,128]{2,1,0:T(8,128)(2,1)S(1)}, bf16[2,128,128]{2,1,0:T(8,128)(2,1)S(1)}, u32[]{:S(2)}, u32[]{:S(2)}) collective-permute-start(bf16[2,128,128]{2,1,0:T(8,128)(2,1)S(1)} %get-tuple-element.83), channel_id=1, source_target_pairs={{0,4},{4,0},{8,12},{12,8},{1,5},{5,1},{9,13},{13,9},{2,6},{6,2},{1... | collective-permute-start | bytes 196616 | tf_op jit(solution)/shard_map/ppermute | solution.py:22
  44.0 0.6 shard_map.84
  44.5 0.3 collective-permute-start.10
  44.8 1.9 %collective-permute-done.9.refs_8_.partner = bf16[2,128,128]{2,1,0:T(8,128)(2,1)S(1)} collective-permute-done((bf16[2,128,128]{2,1,0:T(8,128)(2,1)S(1)}, bf16[2,128,128]{2,1,0:T(8,128)(2,1)S(1)}, u32[]{:S(2)}, u32[]{:S(2)}) %collective-permute-start.9) | collective-permute-done | bytes 65568 | tf_op jit(solution)/shard_map/ppermute | solution.py:22
  46.8 2.8 %collective-permute-start.12 = (bf16[2,128,128]{2,1,0:T(8,128)(2,1)S(1)}, bf16[2,128,128]{2,1,0:T(8,128)(2,1)S(1)}, u32[]{:S(2)}, u32[]{:S(2)}) collective-permute-start(bf16[2,128,128]{2,1,0:T(8,128)(2,1)S(1)} %shard_map.88), channel_id=1, source_target_pairs={{0,8},{4,12},{8,0},{12,4},{1,9},{5,13},{9,1},{13,5},{2,10},{6,14},... | collective-permute-start | bytes 196616 | tf_op jit(solution)/shard_map/ppermute | solution.py:22
  49.6 0.0 collective-permute-done.10.refs_9_.partner
  49.6 2.0 %collective-permute-start.11 = (bf16[2,128,128]{2,1,0:T(8,128)(2,1)S(1)}, bf16[2,128,128]{2,1,0:T(8,128)(2,1)S(1)}, u32[]{:S(2)}, u32[]{:S(2)}) collective-permute-start(bf16[2,128,128]{2,1,0:T(8,128)(2,1)S(1)} %shard_map.87), channel_id=1, source_target_pairs={{0,8},{4,12},{8,0},{12,4},{1,9},{5,13},{9,1},{13,5},{2,10},{6,14},... | collective-permute-start | bytes 196616 | tf_op jit(solution)/shard_map/ppermute | solution.py:22
  51.6 0.0 copy-done.2
  51.6 0.2 shard_map.75.refs_5_
  51.7 0.0 copy-done
  51.7 1.4 %shard_map.82 = (f32[256,512]{1,0:T(8,128)S(1)}, bf16[256,512]{1,0:T(8,128)(2,1)S(1)}, bf16[256,512]{1,0:T(8,128)(2,1)S(1)}) custom-call(bf16[256,512]{1,0:T(8,128)(2,1)S(1)} %collective-permute-done.5.refs_0_, bf16[256,512]{1,0:T(8,128)(2,1)S(1)} %collective-permute-done.6.refs_1_, bf16[2048,512]{1,0:T(8,128)(2,1)S(1)} %get-tuple-element.46.refs_1_.refs_2_, ...), custom_call_target="tpu_custom_call" | custom-call | tf_op jit(solution)/shard_map/pallas_call | solution.py:35
  53.2 1.4 %shard_map.80 = (f32[256,512]{1,0:T(8,128)S(1)}, bf16[256,512]{1,0:T(8,128)(2,1)S(1)}, bf16[256,512]{1,0:T(8,128)(2,1)S(1)}) custom-call(bf16[256,512]{1,0:T(8,128)(2,1)S(1)} %collective-permute-done.3.refs_0_, bf16[256,512]{1,0:T(8,128)(2,1)S(1)} %collective-permute-done.4.refs_1_, bf16[2048,512]{1,0:T(8,128)(2,1)S(1)} %get-tuple-element.46.refs_1_.refs_2_, ...), custom_call_target="tpu_custom_call" | custom-call | tf_op jit(solution)/shard_map/pallas_call | solution.py:35
  54.6 2.2 %shard_map.77 = (f32[384,512]{1,0:T(8,128)S(1)}, bf16[384,512]{1,0:T(8,128)(2,1)S(1)}, bf16[384,512]{1,0:T(8,128)(2,1)S(1)}) custom-call(bf16[384,512]{1,0:T(8,128)(2,1)S(1)} %collective-permute-done.refs_0_, bf16[384,512]{1,0:T(8,128)(2,1)S(1)} %collective-permute-done.1.refs_1_, bf16[2048,512]{1,0:T(8,128)(2,1)S(1)} %get-tuple-element.46.refs_1_.refs_2_, ...), custom_call_target="tpu_custom_call" | custom-call | tf_op jit(solution)/shard_map/pallas_call | solution.py:35
  56.8 1.1 %shard_map.85 = (f32[128,512]{1,0:T(8,128)S(1)}, bf16[128,512]{1,0:T(8,128)(2,1)S(1)}, bf16[128,512]{1,0:T(8,128)(2,1)S(1)}) custom-call(bf16[128,512]{1,0:T(8,128)(2,1)S(1)} %collective-permute-done.7.refs_0_, bf16[128,512]{1,0:T(8,128)(2,1)S(1)} %collective-permute-done.8.refs_1_, bf16[2048,512]{1,0:T(8,128)(2,1)S(1)} %get-tuple-element.46.refs_1_.refs_2_, ...), custom_call_target="tpu_custom_call" | custom-call | tf_op jit(solution)/shard_map/pallas_call | solution.py:35
  58.0 0.0 copy-start.1
  58.0 0.4 shard_map.86.refs_4_
  58.4 0.0 collective-permute-done.12.refs_5_
  58.4 0.2 copy-done.1
  58.6 1.2 %shard_map.89.refs_7_ = bf16[1024,512]{1,0:T(8,128)(2,1)} custom-call(bf16[384,512]{1,0:T(8,128)(2,1)S(1)} %get-tuple-element.57.refs_0_, bf16[256,512]{1,0:T(8,128)(2,1)S(1)} %get-tuple-element.62.refs_1_, bf16[256,512]{1,0:T(8,128)(2,1)S(1)} %get-tuple-element.67.refs_2_, bf16[128,512]{1,0:T(8,128)(2,1)S(1)} %get-tuple-element.74.refs_3_, ...), custom_call_target="tpu_custom_call" | custom-call | tf_op jit(solution)/shard_map/pallas_call | solution.py:35
  59.9 0.0 collective-permute-done.11.refs_5_
  59.9 1.2 %shard_map.90 = bf16[1024,512]{1,0:T(8,128)(2,1)} custom-call(bf16[384,512]{1,0:T(8,128)(2,1)S(1)} %get-tuple-element.57.refs_0_, bf16[256,512]{1,0:T(8,128)(2,1)S(1)} %get-tuple-element.62.refs_1_, bf16[256,512]{1,0:T(8,128)(2,1)S(1)} %get-tuple-element.67.refs_2_, bf16[128,512]{1,0:T(8,128)(2,1)S(1)} %get-tuple-element.74.refs_3_, ...), custom_call_target="tpu_custom_call", output_to_operand_aliasing={{}: (7, {})} | custom-call | tf_op jit(solution)/shard_map/pallas_call | solution.py:35
  (3 shorter events, 0.0 us)
Async XLA Ops:
  0.0 34.6 %collective-permute-start.2 = (bf16[1024,512]{1,0:T(8,128)(2,1)}, bf16[1024,512]{1,0:T(8,128)(2,1)S(1)}, u32[]{:S(2)}, u32[]{:S(2)}) collective-permute-start(bf16[1024,512]{1,0:T(8,128)(2,1)} %tokens.3), channel_id=1, source_target_pairs={{0,1},{1,0},{2,3},{3,2},{4,5},{5,4},{6,7},{7,6},{8,9},{9,8},{10,11... | collective-permute-start | bytes 3145736 | tf_op jit(solution)/shard_map/ppermute | solution.py:22
  1.5 12.5 %collective-permute-start = (bf16[384,512]{1,0:T(8,128)(2,1)S(1)}, bf16[384,512]{1,0:T(8,128)(2,1)S(1)}, u32[]{:S(2)}, u32[]{:S(2)}) collective-permute-start(bf16[384,512]{1,0:T(8,128)(2,1)S(1)} %slice.3), channel_id=1, source_target_pairs={{0,2},{1,3},{2,0},{3,1},{4,6},{5,7},{6,4},{7,5},{8,10},{9,11},{10,... | collective-permute-start | bytes 1179656 | tf_op jit(solution)/shard_map/ppermute | solution.py:22
  5.2 14.5 %collective-permute-start.3 = (bf16[256,512]{1,0:T(8,128)(2,1)S(1)}, bf16[256,512]{1,0:T(8,128)(2,1)S(1)}, u32[]{:S(2)}, u32[]{:S(2)}) collective-permute-start(bf16[256,512]{1,0:T(8,128)(2,1)S(1)} %get-tuple-element.58), channel_id=1, source_target_pairs={{0,2},{1,3},{2,0},{3,1},{4,6},{5,7},{6,4},{7,5},{8,10},{9,11},{10,... | collective-permute-start | bytes 786440 | tf_op jit(solution)/shard_map/ppermute | solution.py:22
  5.2 19.8 %collective-permute-start.5 = (bf16[256,512]{1,0:T(8,128)(2,1)S(1)}, bf16[256,512]{1,0:T(8,128)(2,1)S(1)}, u32[]{:S(2)}, u32[]{:S(2)}) collective-permute-start(bf16[256,512]{1,0:T(8,128)(2,1)S(1)} %get-tuple-element.63), channel_id=1, source_target_pairs={{0,2},{1,3},{2,0},{3,1},{4,6},{5,7},{6,4},{7,5},{8,10},{9,11},{10,... | collective-permute-start | bytes 786440 | tf_op jit(solution)/shard_map/ppermute | solution.py:22
  14.0 22.4 %collective-permute-start.1 = (bf16[384,512]{1,0:T(8,128)(2,1)S(1)}, bf16[384,512]{1,0:T(8,128)(2,1)S(1)}, u32[]{:S(2)}, u32[]{:S(2)}) collective-permute-start(bf16[384,512]{1,0:T(8,128)(2,1)S(1)} %collective-permute-done.refs_0_), channel_id=1, source_target_pairs={{0,1},{1,0},{2,3},{3,2},{4,5},{5,4},{6,7},{7,6},{8,9},{9,8},{10,11... | collective-permute-start | bytes 1179656 | tf_op jit(solution)/shard_map/ppermute | solution.py:22
  19.6 18.7 %collective-permute-start.4 = (bf16[256,512]{1,0:T(8,128)(2,1)S(1)}, bf16[256,512]{1,0:T(8,128)(2,1)S(1)}, u32[]{:S(2)}, u32[]{:S(2)}) collective-permute-start(bf16[256,512]{1,0:T(8,128)(2,1)S(1)} %collective-permute-done.3.refs_0_), channel_id=1, source_target_pairs={{0,1},{1,0},{2,3},{3,2},{4,5},{5,4},{6,7},{7,6},{8,9},{9,8},{10,11... | collective-permute-start | bytes 786440 | tf_op jit(solution)/shard_map/ppermute | solution.py:22
  25.1 14.8 %collective-permute-start.6 = (bf16[256,512]{1,0:T(8,128)(2,1)S(1)}, bf16[256,512]{1,0:T(8,128)(2,1)S(1)}, u32[]{:S(2)}, u32[]{:S(2)}) collective-permute-start(bf16[256,512]{1,0:T(8,128)(2,1)S(1)} %collective-permute-done.5.refs_0_), channel_id=1, source_target_pairs={{0,1},{1,0},{2,3},{3,2},{4,5},{5,4},{6,7},{7,6},{8,9},{9,8},{10,11... | collective-permute-start | bytes 786440 | tf_op jit(solution)/shard_map/ppermute | solution.py:22
  25.1 5.9 %collective-permute-start.7 = (bf16[128,512]{1,0:T(8,128)(2,1)S(1)}, bf16[128,512]{1,0:T(8,128)(2,1)S(1)}, u32[]{:S(2)}, u32[]{:S(2)}) collective-permute-start(bf16[128,512]{1,0:T(8,128)(2,1)S(1)} %get-tuple-element.68), channel_id=1, source_target_pairs={{0,2},{1,3},{2,0},{3,1},{4,6},{5,7},{6,4},{7,5},{8,10},{9,11},{10,... | collective-permute-start | bytes 393224 | tf_op jit(solution)/shard_map/ppermute | solution.py:22
  31.0 10.5 %collective-permute-start.8 = (bf16[128,512]{1,0:T(8,128)(2,1)S(1)}, bf16[128,512]{1,0:T(8,128)(2,1)S(1)}, u32[]{:S(2)}, u32[]{:S(2)}) collective-permute-start(bf16[128,512]{1,0:T(8,128)(2,1)S(1)} %collective-permute-done.7.refs_0_), channel_id=1, source_target_pairs={{0,1},{1,0},{2,3},{3,2},{4,5},{5,4},{6,7},{7,6},{8,9},{9,8},{10,11... | collective-permute-start | bytes 393224 | tf_op jit(solution)/shard_map/ppermute | solution.py:22
  42.1 9.5 %copy-start.2 = (f32[4,16]{1,0:T(4,128)S(1)}, f32[4,16]{1,0:T(4,128)}, u32[]{:S(2)}) copy-start(f32[4,16]{1,0:T(4,128)} %table.1) | copy-start | bytes 772
  42.1 9.7 %copy-start = (s32[6,1024]{1,0:T(8,128)S(1)}, s32[6,1024]{1,0:T(8,128)}, u32[]{:S(2)}) copy-start(s32[6,1024]{1,0:T(8,128)} %refs_4_.7) | copy-start | bytes 73732
  42.1 4.7 %collective-permute-start.9 = (bf16[2,128,128]{2,1,0:T(8,128)(2,1)S(1)}, bf16[2,128,128]{2,1,0:T(8,128)(2,1)S(1)}, u32[]{:S(2)}, u32[]{:S(2)}) collective-permute-start(bf16[2,128,128]{2,1,0:T(8,128)(2,1)S(1)} %get-tuple-element.83), channel_id=1, source_target_pairs={{0,4},{4,0},{8,12},{12,8},{1,5},{5,1},{9,13},{13,9},{2,6},{6,2},{1... | collective-permute-start | bytes 196616 | tf_op jit(solution)/shard_map/ppermute | solution.py:22
  44.5 5.0 %collective-permute-start.10 = (bf16[2,128,128]{2,1,0:T(8,128)(2,1)S(1)}, bf16[2,128,128]{2,1,0:T(8,128)(2,1)S(1)}, u32[]{:S(2)}, u32[]{:S(2)}) collective-permute-start(bf16[2,128,128]{2,1,0:T(8,128)(2,1)S(1)} %get-tuple-element.84), channel_id=1, source_target_pairs={{0,4},{4,0},{8,12},{12,8},{1,5},{5,1},{9,13},{13,9},{2,6},{6,2},{1... | collective-permute-start | bytes 196616 | tf_op jit(solution)/shard_map/ppermute | solution.py:22
  46.8 11.7 %collective-permute-start.12 = (bf16[2,128,128]{2,1,0:T(8,128)(2,1)S(1)}, bf16[2,128,128]{2,1,0:T(8,128)(2,1)S(1)}, u32[]{:S(2)}, u32[]{:S(2)}) collective-permute-start(bf16[2,128,128]{2,1,0:T(8,128)(2,1)S(1)} %shard_map.88), channel_id=1, source_target_pairs={{0,8},{4,12},{8,0},{12,4},{1,9},{5,13},{9,1},{13,5},{2,10},{6,14},... | collective-permute-start | bytes 196616 | tf_op jit(solution)/shard_map/ppermute | solution.py:22
  49.6 10.3 %collective-permute-start.11 = (bf16[2,128,128]{2,1,0:T(8,128)(2,1)S(1)}, bf16[2,128,128]{2,1,0:T(8,128)(2,1)S(1)}, u32[]{:S(2)}, u32[]{:S(2)}) collective-permute-start(bf16[2,128,128]{2,1,0:T(8,128)(2,1)S(1)} %shard_map.87), channel_id=1, source_target_pairs={{0,8},{4,12},{8,0},{12,4},{1,9},{5,13},{9,1},{13,5},{2,10},{6,14},... | collective-permute-start | bytes 196616 | tf_op jit(solution)/shard_map/ppermute | solution.py:22
  58.0 0.7 %copy-start.1 = (f32[512]{0:T(512)S(1)}, f32[512]{0:T(512)}, u32[]{:S(2)}) copy-start(f32[512]{0:T(512)} %param.13) | copy-start | bytes 6148
